TPU v7x, 32 devices: a whole 2x2x4 slice. The times are simulated.
32 devices in a mesh: dp: 4 (over z), ctx: 2 (over core), tensor: 4 (over y, x).
Axes of the slice: x: 2, y: 2, z: 4, core: 2. Of those that a mesh axis runs over, the one named last changes fastest.
Arguments:
- tokens: bfloat16 [4, 1024, 2048], P('dp', 'ctx', 'tensor'), may hold values from -6 to 6
- norm_gain: bfloat16 [2048], P('tensor'), may hold values from 0.5 to 1.5
- inner_weight: bfloat16 [2048, 4096], P(('dp', 'ctx'), 'tensor'), may hold values from -0.125 to 0.125
- gate_weight: bfloat16 [2048, 4096], P(('dp', 'ctx'), 'tensor'), may hold values from -0.125 to 0.125
- conv_weight: float32 [4, 4096], P(None, 'tensor'), may hold values from -3 to 3
- conv_bias: float32 [4096], P('tensor'), may hold values from -3 to 3
- select_weight: bfloat16 [160, 4096], P(('dp', 'ctx'), 'tensor'), may hold values from -0.09375 to 0.09375
- step_weight: bfloat16 [128, 4096], P(('dp', 'ctx'), 'tensor'), may hold values from -0.5 to 0.5
- step_bias: float32 [4096], P('tensor'), may hold values from -7 to -2.5
- log_decay: float32 [16, 4096], P(None, 'tensor'), may hold values from 0 to 2.77
- skip_gain: float32 [4096], P('tensor'), may hold values from 0.5 to 1.5
- out_weight: bfloat16 [4096, 2048], P('tensor', ('dp', 'ctx')), may hold values from -0.1875 to 0.1875
- cotangent: bfloat16 [4, 1024, 2048], P('dp', 'ctx', 'tensor'), may hold values from -6 to 6
Outputs:
- layer_out: float32 [4, 1024, 2048], P('dp', 'ctx', 'tensor')
- tokens_grad: float32 [4, 1024, 2048], P('dp', 'ctx', 'tensor')
- gain_grad: float32 [2048], P('tensor')
- inner_weight_grad: float32 [2048, 4096], P(('dp', 'ctx'), 'tensor')
- gate_weight_grad: float32 [2048, 4096], P(('dp', 'ctx'), 'tensor')
- conv_weight_grad: float32 [4, 4096], P(None, 'tensor')
- conv_bias_grad: float32 [4096], P('tensor')
- select_weight_grad: float32 [160, 4096], P(('dp', 'ctx'), 'tensor')
- step_weight_grad: float32 [128, 4096], P(('dp', 'ctx'), 'tensor')
- step_bias_grad: float32 [4096], P('tensor')
- log_decay_grad: float32 [16, 4096], P(None, 'tensor')
- skip_gain_grad: float32 [4096], P('tensor')
- out_weight_grad: float32 [4096, 2048], P('tensor', ('dp', 'ctx'))
All inputs are finite; a program needn't handle non-finite values.
Results may differ from a plain program's by a relative error of at most 0.012.
Values may be sent and summed in bfloat16 or wider, within the bound.
No kernel may reach another device: no remote copies, remote signals or barrier semaphores. Data moves between devices by JAX's collectives and lax.ppermute only.
A program may use at most 512 MiB of HBM per device.

v0:
```python
import jax
import jax.numpy as jnp
from jax import lax
from jax.sharding import PartitionSpec as P

EPS = 1e-05
GROUP_WIDTH = 16


def from_behind(value, axis, by):
    peers = lax.axis_size(axis)
    pairs = [(i, i + by) for i in range(peers) if 0 <= i + by < peers]
    return lax.ppermute(value, axis, pairs)


def entering(value, axis, combine, identity, reverse):
    peers, position = (lax.axis_size(axis), lax.axis_index(axis))
    everything = jax.tree.map(lambda part: lax.all_gather(part, axis), value)
    start = jax.tree.map(
        lambda part, zero: jnp.broadcast_to(jnp.asarray(zero, part.dtype), part.shape),
        value,
        identity,
    )

    def turn(k, before):
        at = peers - 1 - k if reverse else k
        reached = at > position if reverse else at < position
        new = combine(before, jax.tree.map(lambda part: part[at], everything))
        return jax.tree.map(lambda a, b: jnp.where(reached, a, b), new, before)

    return lax.fori_loop(0, peers, turn, start)


def affine(former, latter):
    return (former[0] * latter[0], latter[0] * former[1] + latter[1])


def moved(values, offset, fill):
    count = values.shape[0]
    filler = jnp.full((abs(offset),) + values.shape[1:], fill, values.dtype)
    if offset > 0:
        return jnp.concatenate([filler, values[: count - offset]], axis=0)
    return jnp.concatenate([values[-offset:], filler], axis=0)


def ordered_scan(factor, driving, reverse):
    length = factor.shape[0]
    rest = factor.shape[1:]
    groups = length // GROUP_WIDTH
    factor_groups = factor.reshape((groups, GROUP_WIDTH) + rest)
    driving_groups = driving.reshape((groups, GROUP_WIDTH) + rest)
    order = list(range(GROUP_WIDTH))
    if reverse:
        order = order[::-1]
    products_list = [None] * GROUP_WIDTH
    states_list = [None] * GROUP_WIDTH
    running_product = factor_groups[:, order[0]]
    running_state = driving_groups[:, order[0]]
    products_list[order[0]] = running_product
    states_list[order[0]] = running_state
    for place in order[1:]:
        current = factor_groups[:, place]
        running_product = current * running_product
        running_state = current * running_state + driving_groups[:, place]
        products_list[place] = running_product
        states_list[place] = running_state
    inside_products = jnp.stack(products_list, axis=1)
    inside_states = jnp.stack(states_list, axis=1)
    whole_product = running_product
    whole_state = running_state
    direction = -1 if reverse else 1
    reach = 1
    while reach < groups:
        earlier_product = moved(whole_product, direction * reach, 1.0)
        earlier_state = moved(whole_state, direction * reach, 0.0)
        whole_product, whole_state = affine(
            (earlier_product, earlier_state), (whole_product, whole_state)
        )
        reach = reach * 2
    entry_product = moved(whole_product, direction, 1.0)
    entry_state = moved(whole_state, direction, 0.0)
    products = inside_products * entry_product[:, None]
    states = inside_states + inside_products * entry_state[:, None]
    return (products.reshape((length,) + rest), states.reshape((length,) + rest))


def silu_slope(values):
    logistic = jax.nn.sigmoid(values)
    return logistic * (1.0 + values * (1.0 - logistic))


def contract(operand, partner):
    return lax.dot_general(
        operand, partner, (((0,), (0,)), ((), ())), preferred_element_type=jnp.float32
    )


def against(operand, partner):
    return lax.dot_general(
        operand, partner, (((1,), (1,)), ((), ())), preferred_element_type=jnp.float32
    )


def shards(
    tokens,
    norm_gain,
    inner_weight,
    gate_weight,
    conv_weight,
    conv_bias,
    select_weight,
    step_weight,
    step_bias,
    log_decay,
    skip_gain,
    out_weight,
    cotangent,
):
    seq_count, local_len, part_width = tokens.shape
    kernel = conv_weight.shape[0]
    state_count = log_decay.shape[0]
    full_tokens, full_gain, full_cot = (
        lax.all_gather(tokens, "tensor", axis=2, tiled=True),
        lax.all_gather(norm_gain, "tensor", axis=0, tiled=True),
        lax.all_gather(cotangent, "tensor", axis=2, tiled=True),
    )
    model_width = full_tokens.shape[2]
    whole_x = full_tokens.astype(jnp.float32)
    gain_full = full_gain.astype(jnp.float32)
    inverse_rms = lax.rsqrt(jnp.mean(whole_x * whole_x, axis=-1, keepdims=True) + EPS)
    normed = (whole_x * inverse_rms * gain_full).astype(jnp.bfloat16).reshape(-1, model_width)
    w_inner, w_gate, w_select, w_step, w_out = (
        lax.all_gather(inner_weight, ("dp", "ctx"), axis=0, tiled=True),
        lax.all_gather(gate_weight, ("dp", "ctx"), axis=0, tiled=True),
        lax.all_gather(select_weight, ("dp", "ctx"), axis=0, tiled=True),
        lax.all_gather(step_weight, ("dp", "ctx"), axis=0, tiled=True),
        lax.all_gather(out_weight, ("dp", "ctx"), axis=1, tiled=True),
    )
    rank_width = w_step.shape[0]
    channels = w_inner.shape[1]
    inner_low = (
        jnp.dot(normed, w_inner, preferred_element_type=jnp.float32)
        .astype(jnp.bfloat16)
        .reshape(seq_count, local_len, channels)
    )
    gate_seq = jnp.dot(normed, w_gate, preferred_element_type=jnp.float32).reshape(
        seq_count, local_len, channels
    )
    edge_rows = inner_low[:, local_len - (kernel - 1) :, :]
    before = from_behind(edge_rows, "ctx", 1)
    extended = jnp.concatenate([before, inner_low], axis=1).astype(jnp.float32)
    conv_pre = conv_bias + conv_weight[0] * extended[:, 0:local_len]
    for offset in range(1, kernel):
        conv_pre = conv_pre + conv_weight[offset] * extended[:, offset : offset + local_len]
    conv_low = jax.nn.silu(conv_pre).astype(jnp.bfloat16).reshape(-1, channels)
    projected = lax.psum(against(conv_low, w_select), "tensor")
    step_in = projected[:, :rank_width].astype(jnp.bfloat16)
    entry_map = projected[:, rank_width : rank_width + state_count]
    read_map = projected[:, rank_width + state_count :]
    step_arg = jnp.dot(step_in, w_step, preferred_element_type=jnp.float32) + step_bias
    step_seq = jax.nn.softplus(step_arg).reshape(seq_count, local_len, channels)
    conv_seq = conv_low.astype(jnp.float32).reshape(seq_count, local_len, channels)
    entry_seq = entry_map.reshape(seq_count, local_len, state_count)
    read_seq = read_map.reshape(seq_count, local_len, state_count)
    decay_rate = -jnp.exp(log_decay)

    def local_states(pieces):
        step_one, entry_one, read_one, conv_one = pieces
        factor = jnp.exp(step_one[:, None, :] * decay_rate[None])
        driving = entry_one[:, :, None] * (step_one * conv_one)[:, None, :]
        products, states = ordered_scan(factor, driving, False)
        return (jnp.sum(read_one[:, :, None] * states, axis=1), products[-1], states[-1])

    local_out, total_decay, end_state = lax.map(
        local_states, (step_seq, entry_seq, read_seq, conv_seq)
    )
    ones_init = jnp.ones_like(total_decay)
    zero_init = jnp.zeros_like(end_state)
    prefix = entering((total_decay, end_state), "ctx", affine, (ones_init, zero_init), False)
    state_in = prefix[1]

    def corrected(pieces):
        step_one, read_one, start_state = pieces
        growth = jnp.exp(jnp.cumsum(step_one[:, None, :] * decay_rate[None], axis=0))
        return jnp.sum(read_one[:, :, None] * growth * start_state[None], axis=1)

    scan_out = local_out + lax.map(corrected, (step_seq, read_seq, state_in)) + skip_gain * conv_seq
    gate_silu = jax.nn.silu(gate_seq)
    gated_low = (scan_out * gate_silu).astype(jnp.bfloat16).reshape(-1, channels)
    out_terms = jnp.dot(gated_low, w_out, preferred_element_type=jnp.float32).reshape(
        seq_count, local_len, model_width
    )
    branch = lax.psum_scatter(out_terms, "tensor", scatter_dimension=2, tiled=True)
    layer_out = tokens.astype(jnp.float32) + branch
    cot_flat = full_cot.reshape(-1, model_width)
    gated_grad = against(cot_flat, w_out).reshape(seq_count, local_len, channels)
    out_full = contract(gated_low, cot_flat)
    y_grad = gated_grad * gate_silu
    gate_grad_low = (
        (gated_grad * scan_out * silu_slope(gate_seq)).astype(jnp.bfloat16).reshape(-1, channels)
    )
    skip_local = jnp.sum(y_grad * conv_seq, axis=(0, 1))

    def first_terms(pieces):
        step_one, read_one, grad_one = pieces
        growth = jnp.exp(jnp.cumsum(step_one[:, None, :] * decay_rate[None], axis=0))
        return jnp.sum(growth * read_one[:, :, None] * grad_one[:, None, :], axis=0)

    first_term = lax.map(first_terms, (step_seq, read_seq, y_grad))
    suffix = entering((total_decay, first_term), "ctx", affine, (ones_init, zero_init), True)
    state_grad_in = suffix[1]

    def gradients(pieces):
        step_one, entry_one, read_one, conv_one, grad_one, start_state, end_grad = pieces
        log_factor = step_one[:, None, :] * decay_rate[None]
        factor = jnp.exp(log_factor)
        driving = entry_one[:, :, None] * (step_one * conv_one)[:, None, :]
        _, states = ordered_scan(factor, driving, False)
        rising = jnp.cumsum(log_factor, axis=0)
        states = states + jnp.exp(rising) * start_state[None]
        earlier_states = jnp.concatenate([start_state[None], states[:-1]], axis=0)
        ahead_factor = jnp.concatenate([factor[1:], jnp.zeros_like(factor[:1])], axis=0)
        source = read_one[:, :, None] * grad_one[:, None, :]
        _, adjoint = ordered_scan(ahead_factor, source, True)
        adjoint = adjoint + jnp.exp(rising[-1][None] - rising) * end_grad[None]
        read_grad = jnp.sum(states * grad_one[:, None, :], axis=2)
        entry_grad = jnp.sum(adjoint * (step_one * conv_one)[:, None, :], axis=2)
        weighted = jnp.sum(adjoint * entry_one[:, :, None], axis=1)
        memory = adjoint * factor * earlier_states
        step_grad = weighted * conv_one + jnp.sum(memory * decay_rate[None], axis=1)
        rate_grad = jnp.sum(memory * step_one[:, None, :], axis=0)
        return (read_grad, entry_grad, weighted * step_one, step_grad, rate_grad)

    read_grad, entry_grad, scan_conv_grad, step_grad, rate_grad = lax.map(
        gradients, (step_seq, entry_seq, read_seq, conv_seq, y_grad, state_in, state_grad_in)
    )
    step_arg_grad = step_grad.reshape(-1, channels) * jax.nn.sigmoid(step_arg)
    step_bias_local = jnp.sum(step_arg_grad, axis=0)
    step_low = step_arg_grad.astype(jnp.bfloat16)
    step_weight_full = contract(step_in, step_low)
    proj_terms = jnp.concatenate(
        [
            against(step_low, w_step),
            entry_grad.reshape(-1, state_count),
            read_grad.reshape(-1, state_count),
        ],
        axis=1,
    )
    proj_grad = lax.psum(proj_terms, "tensor").astype(jnp.bfloat16)
    select_full = contract(proj_grad, conv_low)
    conv_out_grad = (
        scan_conv_grad
        + y_grad * skip_gain
        + jnp.dot(proj_grad, w_select, preferred_element_type=jnp.float32).reshape(
            seq_count, local_len, channels
        )
    )
    conv_pre_grad = conv_out_grad * silu_slope(conv_pre)
    conv_bias_local = jnp.sum(conv_pre_grad, axis=(0, 1))
    conv_weight_local = jnp.stack(
        [
            jnp.sum(conv_pre_grad * extended[:, offset : offset + local_len], axis=(0, 1))
            for offset in range(kernel)
        ]
    )
    extended_grad = jnp.pad(conv_pre_grad * conv_weight[0], ((0, 0), (0, kernel - 1), (0, 0)))
    for offset in range(1, kernel):
        extended_grad = extended_grad + jnp.pad(
            conv_pre_grad * conv_weight[offset], ((0, 0), (offset, kernel - 1 - offset), (0, 0))
        )
    back_edge = from_behind(extended_grad[:, : kernel - 1], "ctx", -1)
    inner_seq_grad = extended_grad[:, kernel - 1 :] + jnp.pad(
        back_edge, ((0, 0), (local_len - kernel + 1, 0), (0, 0))
    )
    inner_grad_low = inner_seq_grad.astype(jnp.bfloat16).reshape(-1, channels)
    inner_full = contract(normed, inner_grad_low)
    gate_full = contract(normed, gate_grad_low)
    normed_terms = (against(inner_grad_low, w_inner) + against(gate_grad_low, w_gate)).reshape(
        seq_count, local_len, model_width
    )
    own_x = tokens.astype(jnp.float32)
    own_gain = norm_gain.astype(jnp.float32)
    normed_full = lax.psum(normed_terms, "tensor")
    token_dots = jnp.sum(normed_full * gain_full * whole_x, axis=-1, keepdims=True)
    column_start = lax.axis_index("tensor") * part_width
    normed_grad = lax.dynamic_slice_in_dim(normed_full, column_start, part_width, 2)
    cubed = inverse_rms * inverse_rms * inverse_rms
    tokens_grad = (
        cotangent.astype(jnp.float32)
        + inverse_rms * own_gain * normed_grad
        - own_x * cubed * token_dots / model_width
    )
    gain_local = jnp.sum(normed_grad * own_x * inverse_rms, axis=(0, 1))
    inner_weight_grad, gate_weight_grad, select_weight_grad, step_weight_grad, out_weight_grad = (
        lax.psum_scatter(inner_full, ("dp", "ctx"), scatter_dimension=0, tiled=True),
        lax.psum_scatter(gate_full, ("dp", "ctx"), scatter_dimension=0, tiled=True),
        lax.psum_scatter(select_full, ("dp", "ctx"), scatter_dimension=0, tiled=True),
        lax.psum_scatter(step_weight_full, ("dp", "ctx"), scatter_dimension=0, tiled=True),
        lax.psum_scatter(out_full, ("dp", "ctx"), scatter_dimension=1, tiled=True),
    )
    gain_grad, conv_weight_grad, conv_bias_grad, step_bias_grad, log_decay_grad, skip_gain_grad = (
        lax.psum(
            (
                gain_local,
                conv_weight_local,
                conv_bias_local,
                step_bias_local,
                jnp.sum(rate_grad, axis=0) * decay_rate,
                skip_local,
            ),
            ("dp", "ctx"),
        )
    )
    return (
        layer_out,
        tokens_grad,
        gain_grad,
        inner_weight_grad,
        gate_weight_grad,
        conv_weight_grad,
        conv_bias_grad,
        select_weight_grad,
        step_weight_grad,
        step_bias_grad,
        log_decay_grad,
        skip_gain_grad,
        out_weight_grad,
    )


def solution(mesh):
    return jax.shard_map(
        shards,
        mesh=mesh,
        in_specs=(
            P("dp", "ctx", "tensor"),
            P("tensor"),
            P(("dp", "ctx"), "tensor"),
            P(("dp", "ctx"), "tensor"),
            P(None, "tensor"),
            P("tensor"),
            P(("dp", "ctx"), "tensor"),
            P(("dp", "ctx"), "tensor"),
            P("tensor"),
            P(None, "tensor"),
            P("tensor"),
            P("tensor", ("dp", "ctx")),
            P("dp", "ctx", "tensor"),
        ),
        out_specs=(
            P("dp", "ctx", "tensor"),
            P("dp", "ctx", "tensor"),
            P("tensor"),
            P(("dp", "ctx"), "tensor"),
            P(("dp", "ctx"), "tensor"),
            P(None, "tensor"),
            P("tensor"),
            P(("dp", "ctx"), "tensor"),
            P(("dp", "ctx"), "tensor"),
            P("tensor"),
            P(None, "tensor"),
            P("tensor"),
            P("tensor", ("dp", "ctx")),
        ),
        check_vma=False,
    )
```

profile of v0, /device:TPU:0, one launch (start us, length us, event | category | flops | bytes accessed | tf_op | source)
XLA Modules:
  0.0 1726.6 jit_solution(6828071585512345572)
XLA Ops:
  10.7 9.5 all-gather.3
  20.2 14.9 all-gather.4
  35.3 12.5 all-gather.11.cloned.1.call-done
  50.6 46.0 %all-gather.13.cloned.1.call-done = bf16[2048,1024]{1,0:T(8,128)(2,1)} async-done(((bf16[256,1024]{1,0:T(8,128)(2,1)}), bf16[2048,1024]{1,0:T(8,128)(2,1)}) %all-gather.13.cloned.1.call-update) | async-done | bytes 4194320 | tf_op jit(solution)/shard_map/all_gather | solution.py:133
  103.3 40.8 %all-gather.15.cloned.1.call-done = bf16[2048,1024]{1,0:T(8,128)(2,1)} async-done(((bf16[256,1024]{1,0:T(8,128)(2,1)}), bf16[2048,1024]{1,0:T(8,128)(2,1)}) %all-gather.15.cloned.1.call-update) | async-done | bytes 4194320 | tf_op jit(solution)/shard_map/all_gather | solution.py:134
  151.6 28.0 %all-gather.19.cloned.1.call-done = bf16[1,512,2048]{2,1,0:T(8,128)(2,1)} async-done(((bf16[1,512,512]{2,1,0:T(8,128)(2,1)}), bf16[1,512,2048]{2,1,0:T(8,128)(2,1)}) %all-gather.19.cloned.1.call-update) | async-done | bytes 2097168 | tf_op jit(solution)/shard_map/all_gather | solution.py:125
  179.7 49.3 %all-gather.17.cloned.1.call-done = bf16[1024,2048]{1,0:T(8,128)(2,1)} async-done(((bf16[1024,256]{1,0:T(8,128)(2,1)}), bf16[1024,2048]{1,0:T(8,128)(2,1)}) %all-gather.17.cloned.1.call-update) | async-done | bytes 4194320 | tf_op jit(solution)/shard_map/all_gather | solution.py:137
  229.0 12.6 fusion.14
  243.2 14.6 all_gather.48
  261.1 24.0 %all-reduce.36.cloned.1.call-done = f32[512,160]{0,1:T(8,128)} async-done(((f32[512,160]{0,1:T(8,128)}), f32[512,160]{0,1:T(8,128)}) %all-reduce.36.cloned.1.call-update) | async-done | bytes 327696 | tf_op jit(solution)/shard_map/psum | solution.py:156
  294.4 11.4 multiply_exponential_fusion
  305.9 11.4 multiply_exponential_fusion.1
  320.0 11.1 copy-done
  332.5 24.4 %bitcast_add_fusion.11 = (f32[32,16,1024]{2,0,1:T(8,128)S(1)}, f32[32,1,16,1024]{3,0,2,1:T(8,128)S(1)}, f32[32,1,16,1024]{3,0,2,1:T(8,128)}, f32[32,1,16,1024]{3...) fusion(f32[32,16,16,1024]{3,0,2,1:T(8,128)} %copy-done, ...), kind=kLoop, calls=%fused_computation.107 | loop fusion | flops 15728640 | bytes 77594624 | tf_op jit(solution)/shard_map/while/body/eval_jaxpr/add | solution.py:64
  356.9 17.5 %multiply_add_fusion.16 = (f32[32,16,1024]{2,0,1:T(8,128)}, f32[32,16,1024]{2,0,1:T(8,128)}, f32[32,1,16,1024]{3,0,2,1:T(8,128)}, f32[32,1,16,1024]{3,0,2,1:T(8,128)}, f32[32,1,16,1024]{3,0,2,1:T(8,128)}) fusion(f32[32,16,1024]{2,0,1:T(8,128)S(1)} %get-tuple-element.479, f32[31,16,1024]{2,0,1:T(8,128)S(1)} %bitcast.344, ...), kind=kLoop, calls=%fused_computation.154 | loop fusion | flops 8912896 | bytes 48168960 | tf_op jit(solution)/shard_map/while/body/eval_jaxpr/add | solution.py:35
  429.7 8.4 constant_dynamic-update-slice_fusion
  442.4 8.8 add_dynamic-update-slice_fusion.1
  492.4 25.4 %slice.669 = f32[511,16,1024]{2,0,1:T(8,128)} slice(f32[512,16,1024]{2,0,1:T(8,128)} %multiply_exponential_fusion), slice={[1:512], [0:16], [0:1024]} | slice | bytes 66977792 | tf_op jit(solution)/shard_map/while/body/eval_jaxpr/slice | solution.py:222
  521.5 23.3 %concatenate.143 = f32[512,16,1024]{2,0,1:T(8,128)} pad(f32[511,16,1024]{2,0,1:T(8,128)} %slice.669, f32[]{:T(128)} %constant.164.clone.1), padding=0_1x0_0x0_0 | pad | bytes 67043332 | tf_op jit(solution)/shard_map/while/body/eval_jaxpr/concatenate | solution.py:222
  544.8 97.3 %fusion.101 = (f32[32,1,16,1024]{3,1,0,2:T(1,128)}, f32[32,1,16,1024]{3,1,0,2:T(1,128)}, f32[32,1,16,1024]{3,1,0,2:T(1,128)}, f32[32,1,16,1024]{3,1,0,2:T(1,128)...) fusion(f32[32,16,16,1024]{3,1,0,2:T(8,128)} %bitcast.340), kind=kLoop, calls=%fused_computation.305 | loop fusion | bytes 67108864 | tf_op jit(solution)/shard_map/while/body/eval_jaxpr/slice | solution.py:57
  645.5 57.2 %multiply_reduce_fusion.7 = (f32[32,16,1024]{2,0,1:T(8,128)}, f32[32,16,16,1024]{3,0,2,1:T(8,128)}, f32[32,16,16,1024]{3,0,2,1:T(8,128)}, f32[32,16,16,1024]{3,0,2,1:T(8,128)}) fusion(f32[32,16,16]{0,2,1:T(8,128)S(1)} %copy.166, f32[32,16,16,1024]{3,0,2,1:T(8,128)} %get-tuple-element.514, f32[32,16,16,1024]{3,0,2,1:T(8,128)} %multiply_dynamic-update-slice_fusion.1, ...), kind=kLoop, calls=%fused_computation.20 | loop fusion | flops 49807360 | bytes 176193536 | tf_op jit(solution)/shard_map/while/body/eval_jaxpr/reduce_sum | solution.py:172
  702.6 25.8 %bitcast_add_fusion.3 = (f32[32,16,1024]{2,0,1:T(8,128)S(1)}, f32[32,1,16,1024]{3,0,2,1:T(8,128)}, f32[32,1,16,1024]{3,0,2,1:T(8,128)}, f32[32,1,16,1024]{3,0,2,...) fusion(f32[32,16,16,1024]{3,0,2,1:T(8,128)} %get-tuple-element.538, ...), kind=kLoop, calls=%fused_computation.75 | loop fusion | flops 15728640 | bytes 77594624 | tf_op jit(solution)/shard_map/while/body/eval_jaxpr/add | solution.py:64
  730.3 20.7 %multiply_add_fusion.6 = (f32[32,16,1024]{2,0,1:T(8,128)}, f32[32,16,1024]{2,0,1:T(8,128)}, f32[32,1,16,1024]{3,0,2,1:T(8,128)}, f32[32,1,16,1024]{3,0,2,1:T(8,1...) fusion(f32[32,16,1024]{2,0,1:T(8,128)} %copy-done.30, f32[31,16,1024]{2,0,1:T(8,128)} %slice.706, ...), kind=kLoop, calls=%fused_computation.136 | loop fusion | flops 8912896 | bytes 50266112 | tf_op jit(solution)/shard_map/while/body/eval_jaxpr/add | solution.py:35
  763.4 17.9 %multiply_dynamic-update-slice_fusion = (f32[32,16,16,1024]{3,0,2,1:T(8,128)}, f32[32,1,16,1024]{3,0,2,1:T(8,128)}, f32[32,1,16,1024]{3,0,2,1:T(8,128)}, f32[32,...) fusion(f32[32,1,16,1024]{3,1,0,2:T(1,128)} %get-tuple-element.5, ...), kind=kLoop, calls=%fused_computation.140 | loop fusion | flops 11010046 | bytes 48234496
  864.0 32.9 %multiply_add_fusion.1 = f32[32,16,16,1024]{3,0,2,1:T(8,128)} fusion(f32[32,16,16,1024]{3,0,2,1:T(8,128)} %slice_dynamic-update-slice_fusion, f32[32,16,16,1024]{3,0,2,1:T(8,128)} %get-tuple-element.549, f32[32,16,1024]{2,0,1:T(8,128)S(1)} %copy-done.55), kind=kLoop, calls=%fused_computation.15 | loop fusion | flops 16777216 | bytes 102760448 | tf_op jit(solution)/shard_map/while/body/eval_jaxpr/add | solution.py:83
  896.8 31.8 %copy.195 = f32[32,16,16,1024]{3,1,0,2:T(8,128)} copy(f32[32,16,16,1024]{3,0,2,1:T(8,128)} %multiply_add_fusion.1) | data formatting | bytes 67108864 | tf_op jit(solution)/shard_map/while/body/eval_jaxpr/add | solution.py:83
  928.6 28.3 %copy.174 = f32[32,16,16,1024]{3,1,0,2:T(8,128)S(1)} copy(f32[32,16,16,1024]{3,0,2,1:T(8,128)} %get-tuple-element.466) | data formatting | bytes 67108864 | tf_op jit(solution)/shard_map/while/body/eval_jaxpr/add | solution.py:83
  958.9 39.1 %copy.173 = f32[32,16,16,1024]{3,2,1,0:T(8,128)} copy(f32[32,16,16,1024]{3,0,2,1:T(8,128)} %get-tuple-element.513) | data formatting | bytes 67108864 | tf_op jit(solution)/shard_map/while/body/eval_jaxpr/mul | solution.py:82
  1003.3 12.1 fusion.3
  1016.4 12.6 broadcast_add_fusion
  1029.1 35.7 %copy.172 = f32[1024,16,4,128]{0,3,2,1:T(8,128)} copy(f32[1024,16,4,128]{0,1,2,3:T(8,128)S(1)} %broadcast_add_fusion) | data formatting | bytes 67108864 | tf_op jit(solution)/shard_map/reduce_window_sum
  1064.8 36.9 %multiply_reduce_fusion.5 = (f32[16,1024]{1,0:T(8,128)S(1)}, f32[512,1024]{1,0:T(8,128)}, f32[512,16]{0,1:T(8,128)}, f32[512,16,1024]{2,0,1:T(8,128)}) fusion(f32[512,1024]{1,0:T(8,128)S(1)} %copy-done.54, f32[512,16]{0,1:T(8,128)S(1)} %copy-done.77, f32[1024,16,4,128]{0,3,2,1:T(8,128)} %copy.172, f32[16,1024]{1,0:T(8,128)S(1)} %bitcast.354, ...), kind=kLoop, calls=%fused_computation.14 | loop fusion | flops 74948608 | bytes 105054208 | tf_op jit(solution)/shard_map/while/body/eval_jaxpr/reduce_sum | solution.py:207
  1108.3 39.2 %multiply_reduce_fusion = (f32[16,1024]{1,0:T(8,128)S(1)}, f32[512,1024]{1,0:T(8,128)}, f32[512,16]{0,1:T(8,128)S(1)}, f32[512,1024]{1,0:T(8,128)}) fusion(f32[512,1024]{1,0:T(8,128)S(1)} %copy-done.21, f32[511,16,1024]{2,0,1:T(8,128)} %bitcast.341, f32[1,16,1024]{2,0,1:T(1,128)S(1)} %copy.197, f32[16,1024]{1,0:T(8,128)S(1)} %copy-done.72, ...), kind=kLoop, calls=%fused_computation.8 | loop fusion | flops 124755968 | bytes 109379584 | tf_op jit(solution)/shard_map/while/body/eval_jaxpr/reduce_sum | solution.py:231
  1154.6 22.4 %all-reduce.41 = bf16[512,160]{0,1:T(8,128)(2,1)} all-reduce(f32[512,160]{0,1:T(8,128)S(1)} %pad_maximum_fusion), channel_id=1, replica_groups=mesh['dp'=4,'ctx'=2,'tensor'=4] {'tensor'}, use_global_device_ids=true, to_apply=%region_16.17 | all-reduce | flops 81920 | bytes 491520 | tf_op jit(solution)/shard_map/psum | solution.py:249
  1177.1 8.2 multiply_reduce_fusion.11
  1198.3 6.5 convolution_bitcast_fusion
  1207.6 7.9 fusion.90
  1216.7 7.5 fusion.29
  1225.8 7.4 fusion.80
  1236.3 21.3 %fusion = f32[24,1024]{1,0:T(8,128)S(1)} fusion(f32[160,1024]{1,0:T(8,128)} %fusion.57), kind=kCustom, calls=%all-reduce-scatter | all-reduce-scatter fusion | flops 196609 | bytes 754176
  1262.7 38.2 %all-reduce.38.cloned.1.call-done = f32[1,512,2048]{2,1,0:T(8,128)} async-done(((f32[1,512,2048]{2,1,0:T(8,128)}), f32[1,512,2048]{2,1,0:T(8,128)}) %all-reduce.38.cloned.1.call-update) | async-done | bytes 4194320 | tf_op jit(solution)/shard_map/psum | solution.py:283
  1303.6 52.8 %reduce-scatter.8.cloned.1.call-done = f32[1,512,512]{2,1,0:T(8,128)} async-done(((f32[1,512,2048]{2,1,0:T(8,128)}), f32[1,512,512]{2,1,0:T(8,128)}) %reduce-scatter.8.cloned.1.call-update) | async-done | bytes 1048592 | tf_op jit(solution)/shard_map/reduce_scatter | solution.py:193
  1359.8 29.2 %all-reduce.30 = (f32[512]{0:T(512)}, f32[4,1024]{1,0:T(4,128)}, f32[1024]{0:T(1024)}, f32[1024]{0:T(1024)}, f32[1024]{0:T(1024)}) all-reduce(f32[512]{0:T(512)S(1)} %get-tuple-element.523, f32[4,1024]{1,0:T(4,128)S(1)} %pad_maximum_fusion.1, ...), channel_id=1, replica_groups=mesh['dp'=4,'ctx'=2,'tensor'=4] {'dp','ctx'}, use_global_device_ids=true, to_apply=%region_20.21 | all-reduce | flops 7680 | bytes 61440 | tf_op jit(solution)/shard_map/psum | solution.py:302
  1389.0 24.1 %all-reduce.40.cloned.1.call-done = f32[16,1024]{1,0:T(8,128)} async-done(((f32[16,1024]{1,0:T(8,128)}), f32[16,1024]{1,0:T(8,128)}) %all-reduce.40.cloned.1.call-update) | async-done | bytes 65552 | tf_op jit(solution)/shard_map/psum | solution.py:302
  1413.1 32.7 %reduce-scatter.14.cloned.1.call-done = f32[16,1024]{1,0:T(8,128)} async-done(((f32[128,1024]{1,0:T(8,128)}), f32[16,1024]{1,0:T(8,128)}) %reduce-scatter.14.cloned.1.call-update) | async-done | bytes 65552 | tf_op jit(solution)/shard_map/reduce_scatter | solution.py:298
  1445.8 90.8 %reduce-scatter.12.cloned.1.call-done = f32[256,1024]{1,0:T(8,128)} async-done(((f32[2048,1024]{1,0:T(8,128)}), f32[256,1024]{1,0:T(8,128)}) %reduce-scatter.12.cloned.1.call-update) | async-done | bytes 1048592 | tf_op jit(solution)/shard_map/reduce_scatter | solution.py:296
  1536.6 90.8 %reduce-scatter.16.cloned.1.call-done = f32[1024,256]{1,0:T(8,128)} async-done(((f32[1024,2048]{1,0:T(8,128)}), f32[1024,256]{1,0:T(8,128)}) %reduce-scatter.16.cloned.1.call-update) | async-done | bytes 1048592 | tf_op jit(solution)/shard_map/reduce_scatter | solution.py:299
  1627.4 91.0 %reduce-scatter.10.cloned.1.call-done = f32[256,1024]{1,0:T(8,128)} async-done(((f32[2048,1024]{1,0:T(8,128)}), f32[256,1024]{1,0:T(8,128)}) %reduce-scatter.10.cloned.1.call-update) | async-done | bytes 1048592 | tf_op jit(solution)/shard_map/reduce_scatter | solution.py:295
  (405 shorter events, 298.8 us)
Async XLA Ops:
  7.2 40.6 %all-gather.11.cloned.1.call-start = ((), (), s32[]{:S(2)}) async-start(), calls=%async_computation.5 | async-start | bytes 2621440 | tf_op jit(solution)/shard_map/all_gather | solution.py:123
  7.9 88.6 %all-gather.13.cloned.1.call-start = ((), (), s32[]{:S(2)}) async-start(), calls=%async_computation.6 | async-start | bytes 4718592 | tf_op jit(solution)/shard_map/all_gather | solution.py:133
  8.7 135.4 %all-gather.15.cloned.1.call-start = ((), (), s32[]{:S(2)}) async-start(), calls=%async_computation.8 | async-start | bytes 4718592 | tf_op jit(solution)/shard_map/all_gather | solution.py:134
  9.4 170.2 %all-gather.19.cloned.1.call-start = ((), (), s32[]{:S(2)}) async-start(), calls=%async_computation.11 | async-start | bytes 2621440 | tf_op jit(solution)/shard_map/all_gather | solution.py:125
  10.0 218.9 %all-gather.17.cloned.1.call-start = ((), (), s32[]{:S(2)}) async-start(), calls=%async_computation.9 | async-start | bytes 4718592 | tf_op jit(solution)/shard_map/all_gather | solution.py:137
  10.6 274.5 %all-reduce.36.cloned.1.call-start = ((), (), s32[]{:S(2)}) async-start(), calls=%async_computation.7 | async-start | bytes 655360 | tf_op jit(solution)/shard_map/psum | solution.py:156
  20.2 123.8 %copy-start.85 = (f32[4,1,512]{2,1,0:T(1,128)}, f32[4,1,512]{2,1,0:T(1,128)S(1)}, u32[]{:S(2)}) copy-start(f32[4,1,512]{2,1,0:T(1,128)S(1)} %convert_element_type.83) | copy-start | bytes 24580
  35.2 206.4 %copy-start.66 = (bf16[160,1024]{1,0:T(8,128)(2,1)}, bf16[160,1024]{1,0:T(8,128)(2,1)S(1)}, u32[]{:S(2)}) copy-start(bf16[160,1024]{1,0:T(8,128)(2,1)S(1)} %reshape.352) | copy-start | bytes 983044
  35.3 193.7 %copy-start.95 = (f32[1,1024]{1,0:T(1,128)}, f32[1,1024]{1,0:T(1,128)S(1)}, u32[]{:S(2)}) copy-start(f32[1,1024]{1,0:T(1,128)S(1)} %get-tuple-element.541) | copy-start | bytes 12292
  35.3 193.7 %copy-start.97 = (f32[1,1024]{1,0:T(1,128)}, f32[1,1024]{1,0:T(1,128)S(1)}, u32[]{:S(2)}) copy-start(f32[1,1024]{1,0:T(1,128)S(1)} %get-tuple-element.542) | copy-start | bytes 12292
  35.3 193.7 %copy-start.99 = (f32[1,1024]{1,0:T(1,128)}, f32[1,1024]{1,0:T(1,128)S(1)}, u32[]{:S(2)}) copy-start(f32[1,1024]{1,0:T(1,128)S(1)} %get-tuple-element.543) | copy-start | bytes 12292
  35.3 193.7 %copy-start.100 = (f32[1,1024]{1,0:T(1,128)}, f32[1,1024]{1,0:T(1,128)S(1)}, u32[]{:S(2)}) copy-start(f32[1,1024]{1,0:T(1,128)S(1)} %get-tuple-element.544) | copy-start | bytes 12292
  47.8 48.8 %copy-start.51 = (bf16[1,512,2048]{2,1,0:T(8,128)(2,1)S(1)}, bf16[1,512,2048]{2,1,0:T(8,128)(2,1)}, u32[]{:S(2)}) copy-start(bf16[1,512,2048]{2,1,0:T(8,128)(2,1)} %all-gather.11.cloned.1.call-done) | copy-start | bytes 6291460
  50.6 93.5 %copy-start.89 = (f32[512]{0:T(512)}, f32[512]{0:T(512)S(1)}, u32[]{:S(2)}) copy-start(f32[512]{0:T(512)S(1)} %get-tuple-element.546) | copy-start | bytes 6148
  101.1 48.9 %collective-permute-start = (bf16[1,3,1024]{2,1,0:T(4,128)(2,1)S(1)}, bf16[1,3,1024]{2,1,0:T(4,128)(2,1)S(1)}, u32[]{:S(2)}, u32[]{:S(2)}) collective-permute-start(bf16[1,3,1024]{2,1,0:T(4,128)(2,1)S(1)} %slice.612), channel_id=1, source_target_pairs={{0,4},{1,5},{2,6},{3,7},{8,12},{9,13},{10,14},{11,15},{16,20},{17,... | collective-permute-start | bytes 18440 | tf_op jit(solution)/shard_map/ppermute | solution.py:13
  150.0 79.0 %copy-start.104 = (f32[1024]{0:T(1024)S(1)}, f32[1024]{0:T(1024)}, u32[]{:S(2)}) copy-start(f32[1024]{0:T(1024)} %param.22) | copy-start | bytes 12292
  241.6 43.5 %copy-start.42 = (bf16[1,512,1024]{2,1,0:T(8,128)(2,1)}, bf16[1,512,1024]{2,1,0:T(8,128)(2,1)S(1)}, u32[]{:S(2)}) copy-start(bf16[1,512,1024]{2,1,0:T(8,128)(2,1)S(1)} %get-tuple-element.436) | copy-start | bytes 3145732
  243.2 1057.6 %all-reduce.38.cloned.1.call-start = ((), (), s32[]{:S(2)}) async-start(), calls=%async_computation.12 | async-start | bytes 8388608 | tf_op jit(solution)/shard_map/psum | solution.py:283
  258.5 47.4 %copy-start.71 = (f32[16,1024]{1,0:T(8,128)}, f32[16,1024]{1,0:T(8,128)S(1)}, u32[]{:S(2)}) copy-start(f32[16,1024]{1,0:T(8,128)S(1)} %get-tuple-element.539) | copy-start | bytes 196612
  292.3 199.8 %copy-start.76 = (f32[512,16]{0,1:T(8,128)}, f32[512,16]{0,1:T(8,128)S(1)}, u32[]{:S(2)}) copy-start(f32[512,16]{0,1:T(8,128)S(1)} %get-tuple-element.537) | copy-start | bytes 98308
  429.7 39.5 %slice-start = ((s8[33554432]{0:T(1024)(128)(4,1)}), s8[4194304]{0:T(1024)(128)(4,1)S(1)}, s32[]{:S(2)}) async-start(s8[33554432]{0:T(1024)(128)(4,1)} %bitcast.336), calls=%async_computation.18 | async-start | bytes 8388608
  429.7 39.5 %slice-start.1 = ((s8[33554432]{0:T(1024)(128)(4,1)}), s8[4194304]{0:T(1024)(128)(4,1)S(1)}, s32[]{:S(2)}) async-start(s8[33554432]{0:T(1024)(128)(4,1)} %bitcast.336), calls=%async_computation.19 | async-start | bytes 8388608
  645.5 57.2 %copy-start.2 = (f32[32,1,16,1024]{3,1,0,2:T(1,128)S(1)}, f32[32,1,16,1024]{3,1,0,2:T(1,128)}, u32[]{:S(2)}) copy-start(f32[32,1,16,1024]{3,1,0,2:T(1,128)} %get-tuple-element.509) | copy-start | bytes 6291460
  956.9 41.1 %copy-start.1 = (f32[32,16,16,1024]{3,1,0,2:T(8,128)}, f32[32,16,16,1024]{3,1,0,2:T(8,128)S(1)}, u32[]{:S(2)}) copy-start(f32[32,16,16,1024]{3,1,0,2:T(8,128)S(1)} %copy.174) | copy-start | bytes 100663296
  958.9 41.8 %copy-start.59 = (f32[1,16,1024]{2,1,0:T(8,128)S(1)}, f32[1,16,1024]{2,1,0:T(8,128)}, u32[]{:S(2)}) copy-start(f32[1,16,1024]{2,1,0:T(8,128)} %custom-call) | copy-start | bytes 196612
  958.9 41.9 %copy-start.22 = (f32[512,1024]{1,0:T(8,128)S(1)}, f32[512,1024]{1,0:T(8,128)}, u32[]{:S(2)}) copy-start(f32[512,1024]{1,0:T(8,128)} %get-tuple-element.548) | copy-start | bytes 6291460
  958.9 41.9 %copy-start.84 = (f32[1024]{0:T(1024)S(1)}, f32[1024]{0:T(1024)}, u32[]{:S(2)}) copy-start(f32[1024]{0:T(1024)} %param.25) | copy-start | bytes 12292
  1029.0 35.8 %copy-start.54 = (f32[512,1024]{1,0:T(8,128)S(1)}, f32[512,1024]{1,0:T(8,128)}, u32[]{:S(2)}) copy-start(f32[512,1024]{1,0:T(8,128)} %copy-done.53) | copy-start | bytes 6291460
  1029.0 35.8 %copy-start.77 = (f32[512,16]{0,1:T(8,128)S(1)}, f32[512,16]{0,1:T(8,128)}, u32[]{:S(2)}) copy-start(f32[512,16]{0,1:T(8,128)} %copy-done.76) | copy-start | bytes 98308
  1064.8 38.8 %copy-start.62 = (f32[1,16,1024]{2,1,0:T(8,128)S(1)}, f32[1,16,1024]{2,1,0:T(8,128)}, u32[]{:S(2)}) copy-start(f32[1,16,1024]{2,1,0:T(8,128)} %custom-call.1) | copy-start | bytes 196612
  1064.8 43.4 %copy-start.72 = (f32[16,1024]{1,0:T(8,128)S(1)}, f32[16,1024]{1,0:T(8,128)}, u32[]{:S(2)}) copy-start(f32[16,1024]{1,0:T(8,128)} %copy-done.71) | copy-start | bytes 196612
  1064.8 43.4 %copy-start.75 = (f32[512,16]{0,1:T(8,128)S(1)}, f32[512,16]{0,1:T(8,128)}, u32[]{:S(2)}) copy-start(f32[512,16]{0,1:T(8,128)} %copy-done.74) | copy-start | bytes 98308
  1108.3 39.3 %copy-start.23 = (f32[512,1024]{1,0:T(8,128)S(1)}, f32[512,1024]{1,0:T(8,128)}, u32[]{:S(2)}) copy-start(f32[512,1024]{1,0:T(8,128)} %get-tuple-element.548) | copy-start | bytes 6291460
  1108.3 39.3 %copy-start.43 = (bf16[1,512,1024]{2,1,0:T(8,128)(2,1)S(1)}, bf16[1,512,1024]{2,1,0:T(8,128)(2,1)}, u32[]{:S(2)}) copy-start(bf16[1,512,1024]{2,1,0:T(8,128)(2,1)} %copy-done.42) | copy-start | bytes 3145732
  1108.3 39.3 %copy-start.50 = (f32[512,1024]{1,0:T(8,128)S(1)}, f32[512,1024]{1,0:T(8,128)}, u32[]{:S(2)}) copy-start(f32[512,1024]{1,0:T(8,128)} %get-tuple-element.400) | copy-start | bytes 6291460
  1108.3 39.2 %copy-start.91 = (f32[1024]{0:T(1024)S(1)}, f32[1024]{0:T(1024)}, u32[]{:S(2)}) copy-start(f32[1024]{0:T(1024)} %param.27) | copy-start | bytes 12292
  1185.3 6.1 collective-permute-start.1
  1197.1 159.4 %reduce-scatter.8.cloned.1.call-start = ((), (), s32[]{:S(2)}) async-start(), calls=%async_computation.10 | async-start | bytes 5242880 | tf_op jit(solution)/shard_map/reduce_scatter | solution.py:193
  1204.8 208.3 %all-reduce.40.cloned.1.call-start = ((), (), s32[]{:S(2)}) async-start(), calls=%async_computation.16 | async-start | bytes 131072 | tf_op jit(solution)/shard_map/psum | solution.py:302
  1206.3 239.5 %reduce-scatter.14.cloned.1.call-start = ((), (), s32[]{:S(2)}) async-start(), calls=%async_computation.15 | async-start | bytes 589824 | tf_op jit(solution)/shard_map/reduce_scatter | solution.py:298
  1207.5 329.1 %reduce-scatter.12.cloned.1.call-start = ((), (), s32[]{:S(2)}) async-start(), calls=%async_computation.14 | async-start | bytes 9437184 | tf_op jit(solution)/shard_map/reduce_scatter | solution.py:296
  1215.5 411.9 %reduce-scatter.16.cloned.1.call-start = ((), (), s32[]{:S(2)}) async-start(), calls=%async_computation.17 | async-start | bytes 9437184 | tf_op jit(solution)/shard_map/reduce_scatter | solution.py:299
  1224.2 494.2 %reduce-scatter.10.cloned.1.call-start = ((), (), s32[]{:S(2)}) async-start(), calls=%async_computation.13 | async-start | bytes 9437184 | tf_op jit(solution)/shard_map/reduce_scatter | solution.py:295
  1257.6 4.0 collective-permute-start.2
  1258.9 2.7 collective-permute-start.3
  1262.7 93.8 %copy-start.64 = (bf16[1,512,512]{2,1,0:T(8,128)(2,1)S(1)}, bf16[1,512,512]{2,1,0:T(8,128)(2,1)}, u32[]{:S(2)}) copy-start(bf16[1,512,512]{2,1,0:T(8,128)(2,1)} %param.17) | copy-start | bytes 1572868
  1262.7 93.8 %copy-start.65 = (bf16[1,512,512]{2,1,0:T(8,128)(2,1)S(1)}, bf16[1,512,512]{2,1,0:T(8,128)(2,1)}, u32[]{:S(2)}) copy-start(bf16[1,512,512]{2,1,0:T(8,128)(2,1)} %param.29) | copy-start | bytes 1572868
  1262.7 93.8 %copy-start.88 = (f32[512]{0:T(512)S(1)}, f32[512]{0:T(512)}, u32[]{:S(2)}) copy-start(f32[512]{0:T(512)} %get-tuple-element.545) | copy-start | bytes 6148
  (83 other events, 560.6 us)
Sparse Core Ops, SparseCore 0:
  9.9 37.8 all-gather.10
  49.4 47.1 all-gather.12
  98.2 45.8 all-gather.14
  145.7 33.8 all-gather.18
  181.1 47.7 all-gather.16
  243.3 41.7 all-reduce.35
  1197.2 103.5 all-reduce.37
  1303.8 52.6 reduce-scatter.7
  1359.5 53.5 all-reduce.39
  1415.8 29.9 reduce-scatter.13
  1448.7 87.7 reduce-scatter.11
  1539.4 87.9 reduce-scatter.15
  1630.4 87.9 reduce-scatter.9
where the time goes:
time: 1740 us; the launch traced here: 1730 us
  waiting for transfers between devices  626 us (36%)
  other arithmetic  493 us (28%)
  local copies, waits for them, and re-layouts  391 us (22%)
  blocking collectives  118 us (7%)
  matrix products  75.4 us (4%)
    unnamed x35, other arithmetic  135 us
    slice x1, local copies, waits for them, and re-layouts, ordered_scan(): running_product = factor_groups[:, order[0]]  97.3 us
    reduce_scatter x1, waiting for transfers between devices, shards(): lax.psum_scatter(inner_full, ('dp', 'ctx'), scatter_dimension=0, tiled=True)  91 us
    reduce_scatter x1, waiting for transfers between devices, shards(): lax.psum_scatter(gate_full, ('dp', 'ctx'), scatter_dimension=0, tiled=True)  90.8 us
    reduce_scatter x1, waiting for transfers between devices, shards(): lax.psum_scatter(out_full, ('dp', 'ctx'), scatter_dimension=1, tiled=True)  90.8 us
    unnamed x257, local copies, waits for them, and re-layouts  80.3 us
    add x2, local copies, waits for them, and re-layouts, ordered_scan(): states = inside_states + inside_products * entry_state[:, None]  60 us
    reduce_sum x1, other arithmetic, local_states(): jnp.sum(read_one[:, :, None] * states, axis=1)  57.2 us
  transfers between devices with their start and end apart: 17, of which 14 were waited for; matrix products, arithmetic and copies ran while one was open for 5% of the time, Pallas kernels for 0%

commit v1 on v0

v1 whole, which is shorter than its diff:
```python
import functools

import jax
import jax.numpy as jnp
from jax import lax
from jax.experimental import pallas as pl
from jax.experimental.pallas import tpu as pltpu
from jax.sharding import PartitionSpec as P

EPS = 1e-05
LOG2E = 1.4426950408889634
LN2 = 0.6931471805599453
LANES = 128
SUB = 8
TIME_BLOCK = 128
F32 = jnp.float32
BF16 = jnp.bfloat16


def silu_slope(values):
    logistic = jax.nn.sigmoid(values)
    return logistic * (1.0 + values * (1.0 - logistic))


def contract(operand, partner):
    return lax.dot_general(
        operand, partner, (((0,), (0,)), ((), ())), preferred_element_type=F32
    )


def against(operand, partner):
    return lax.dot_general(
        operand, partner, (((1,), (1,)), ((), ())), preferred_element_type=F32
    )


def matmul(operand, partner):
    return jnp.dot(operand, partner, preferred_element_type=F32)


def swap(value, axis, offset):
    peers = lax.axis_size(axis)
    return lax.ppermute(value, axis, [(i, i ^ offset) for i in range(peers)])


def gather_pieces(value, axis):
    return [value] + [swap(value, axis, k) for k in range(1, lax.axis_size(axis))]


def stacked(pieces, axis):
    me = lax.axis_index(axis)
    out = jnp.zeros((len(pieces),) + pieces[0].shape, pieces[0].dtype)
    for k, piece in enumerate(pieces):
        out = lax.dynamic_update_slice_in_dim(out, piece[None], me ^ k, 0)
    return out


def exchange_sum(blocks_of, axis):
    me = lax.axis_index(axis)
    total = blocks_of(me).astype(F32)
    for k in range(1, lax.axis_size(axis)):
        total = total + swap(blocks_of(me ^ k), axis, k).astype(F32)
    return total


def everyone_sum(value, axis):
    total = value.astype(F32)
    for k in range(1, lax.axis_size(axis)):
        total = total + swap(value, axis, k).astype(F32)
    return total


def in_order(mine, other, position, axis):
    return jnp.where(
        position == 0,
        jnp.concatenate([mine, other], axis=axis),
        jnp.concatenate([other, mine], axis=axis),
    )


def half_of(value, which, axis):
    size = value.shape[axis] // 2
    return lax.dynamic_slice_in_dim(value, which * size, size, axis)


def assemble_kernel(count, order_ref, *refs):
    pieces, out_ref = refs[:count], refs[count]
    width = pieces[0].shape[1]
    for k in range(count):
        start = pl.multiple_of(order_ref[k] * width, LANES)
        out_ref[:, pl.ds(start, width)] = pieces[k][...]


def norm_kernel(count, total_width, order_ref, *refs):
    pieces, gains = refs[:count], refs[count : 2 * count]
    out_ref, inv_ref = refs[2 * count :]
    width = pieces[0].shape[1]
    total = None
    for k in range(count):
        part = pieces[k][...].astype(F32)
        squares = jnp.sum(part * part, axis=1, keepdims=True)
        total = squares if total is None else total + squares
    inverse = lax.rsqrt(total / total_width + EPS)
    inv_ref[...] = inverse
    for k in range(count):
        start = pl.multiple_of(order_ref[k] * width, LANES)
        normed = pieces[k][...].astype(F32) * inverse * gains[k][...].astype(F32)
        out_ref[:, pl.ds(start, width)] = normed.astype(BF16)


def row_block(rows):
    for size in (128, 64, 32, 16):
        if rows % size == 0:
            return size
    return rows


def assembled(pieces, order):
    rows, width = pieces[0].shape
    count = len(pieces)
    block = row_block(rows)
    return pl.pallas_call(
        functools.partial(assemble_kernel, count),
        grid_spec=pltpu.PrefetchScalarGridSpec(
            num_scalar_prefetch=1,
            grid=(rows // block,),
            in_specs=[pl.BlockSpec((block, width), lambda i, o: (i, 0))] * count,
            out_specs=pl.BlockSpec((block, width * count), lambda i, o: (i, 0)),
        ),
        out_shape=jax.ShapeDtypeStruct((rows, width * count), pieces[0].dtype),
        name="assemble",
    )(order, *pieces)


def normalized(pieces, gains, order):
    rows, width = pieces[0].shape
    count = len(pieces)
    block = row_block(rows)
    return pl.pallas_call(
        functools.partial(norm_kernel, count, float(width * count)),
        grid_spec=pltpu.PrefetchScalarGridSpec(
            num_scalar_prefetch=1,
            grid=(rows // block,),
            in_specs=[pl.BlockSpec((block, width), lambda i, o: (i, 0))] * count
            + [pl.BlockSpec((1, width), lambda i, o: (0, 0))] * count,
            out_specs=[
                pl.BlockSpec((block, width * count), lambda i, o: (i, 0)),
                pl.BlockSpec((block, 1), lambda i, o: (i, 0)),
            ],
        ),
        out_shape=[
            jax.ShapeDtypeStruct((rows, width * count), BF16),
            jax.ShapeDtypeStruct((rows, 1), F32),
        ],
        name="normalize",
    )(order, *pieces, *gains)


def row_of(ref, t, l):
    return ref[l, pl.ds(t, SUB, stride=0), :]


def spread(ref, values):
    for l in range(ref.shape[0]):
        ref[l] = values[:, l * LANES : (l + 1) * LANES]


def columns_of(values, j):
    return [
        jnp.broadcast_to(values[s : s + SUB, j : j + 1], (SUB, LANES))
        for s in range(0, values.shape[0], SUB)
    ]


def fold_rows(ref, count, l):
    total = ref[l, pl.ds(0, count, stride=SUB), :]
    for s in range(1, SUB):
        total = total + ref[l, pl.ds(s, count, stride=SUB), :]
    return total


def scan_kernel(
    dt_ref, x_ref, bt_ref, ct_ref, rate_ref, y_ref, start_ref, state, dt_rows, u_rows, part
):
    states, width = state.shape
    steps = dt_ref.shape[0]
    slices = [pl.ds(l, LANES) for l in range(0, width, LANES)]
    halves = [pl.ds(s, SUB) for s in range(0, states, SUB)]

    @pl.when(pl.program_id(0) == 0)
    def _():
        state[...] = jnp.zeros_like(state)

    start_ref[0] = state[...]
    spread(dt_rows, dt_ref[...])
    spread(u_rows, dt_ref[...] * x_ref[...].astype(F32))
    rates = [[rate_ref[h, l] for h in halves] for l in slices]

    def group(g, carried):
        base = pl.multiple_of(g * SUB, SUB)
        away = lax.rem(steps - base, steps)
        b_near = pltpu.roll(bt_ref[...], away, 1)
        c_near = pltpu.roll(ct_ref[...], away, 1)
        now = [list(one) for one in carried]
        for j in range(SUB):
            entry, read = columns_of(b_near, j), columns_of(c_near, j)
            row = pl.multiple_of((base + j) * SUB, SUB)
            for l, lanes in enumerate(slices):
                dt = row_of(dt_rows, base + j, l)
                u = row_of(u_rows, base + j, l)
                out = None
                for h in range(len(halves)):
                    new = jnp.exp2(dt * rates[l][h]) * now[l][h] + entry[h] * u
                    now[l][h] = new
                    term = read[h] * new
                    out = term if out is None else out + term
                part[l, pl.ds(row, SUB), :] = out
        return tuple(tuple(one) for one in now)

    first = tuple(tuple(state[h, l] for h in halves) for l in slices)
    last = lax.fori_loop(0, steps // SUB, group, first)
    for l, lanes in enumerate(slices):
        for h, rows in enumerate(halves):
            state[rows, lanes] = last[l][h]
        y_ref[:, lanes] = fold_rows(part, steps, l)


def scanned(dt, x, entry_t, read_t, rate):
    length, width = dt.shape
    states = rate.shape[0]
    block = TIME_BLOCK
    count = length // block
    groups = width // LANES
    by_time = pl.BlockSpec((block, width), lambda i: (i, 0))
    across = pl.BlockSpec((states, block), lambda i: (0, i))
    return pl.pallas_call(
        scan_kernel,
        grid=(count,),
        in_specs=[
            by_time,
            by_time,
            across,
            across,
            pl.BlockSpec((states, width), lambda i: (0, 0)),
        ],
        out_specs=[by_time, pl.BlockSpec((1, states, width), lambda i: (i, 0, 0))],
        out_shape=[
            jax.ShapeDtypeStruct((length, width), F32),
            jax.ShapeDtypeStruct((count, states, width), F32),
        ],
        scratch_shapes=[
            pltpu.VMEM((states, width), F32),
            pltpu.VMEM((groups, block, LANES), F32),
            pltpu.VMEM((groups, block, LANES), F32),
            pltpu.VMEM((groups, block * SUB, LANES), F32),
        ],
        name="scan_forward",
    )(dt, x, entry_t, read_t, rate)


def back_kernel(
    dt_ref,
    x_ref,
    grad_ref,
    bt_ref,
    ct_ref,
    rate_ref,
    start_ref,
    conv_ref,
    step_ref,
    entry_ref,
    read_ref,
    rate_grad_ref,
    ahead,
    dt_rows,
    u_rows,
    grad_rows,
    factors,
    levels,
    weighted,
    memory,
    entry_part,
    read_part,
):
    states, width = ahead.shape
    steps = dt_ref.shape[0]
    slices = [pl.ds(l, LANES) for l in range(0, width, LANES)]
    halves = [pl.ds(s, SUB) for s in range(0, states, SUB)]

    @pl.when(pl.program_id(0) == 0)
    def _():
        ahead[...] = jnp.zeros_like(ahead)
        rate_grad_ref[...] = jnp.zeros_like(rate_grad_ref)

    spread(dt_rows, dt_ref[...])
    spread(u_rows, dt_ref[...] * x_ref[...].astype(F32))
    spread(grad_rows, grad_ref[...])
    rates = [[rate_ref[h, l] for h in halves] for l in slices]
    levels[pl.ds(0, states), :] = start_ref[0]

    def rise(g, carried):
        base = pl.multiple_of(g * SUB, SUB)
        b_near = pltpu.roll(bt_ref[...], lax.rem(steps - base, steps), 1)
        now = [list(one) for one in carried]
        for j in range(SUB):
            entry = columns_of(b_near, j)
            row = pl.multiple_of((base + j) * states, states)
            for l, lanes in enumerate(slices):
                dt = row_of(dt_rows, base + j, l)
                u = row_of(u_rows, base + j, l)
                for h in range(len(halves)):
                    factor = jnp.exp2(dt * rates[l][h])
                    new = factor * now[l][h] + entry[h] * u
                    now[l][h] = new
                    factors[pl.ds(row + h * SUB, SUB), lanes] = factor
                    levels[pl.ds(row + states + h * SUB, SUB), lanes] = new
        return tuple(tuple(one) for one in now)

    first = tuple(tuple(start_ref[0, h, l] for h in halves) for l in slices)
    top = lax.fori_loop(0, steps // SUB, rise, first)

    def fall(k, carried):
        base = pl.multiple_of(steps - SUB - k * SUB, SUB)
        away = lax.rem(steps - base, steps)
        b_near = pltpu.roll(bt_ref[...], away, 1)
        c_near = pltpu.roll(ct_ref[...], away, 1)
        near, level, rate_sum = ([list(one) for one in part] for part in carried)
        for j in range(SUB - 1, -1, -1):
            entry, read = columns_of(b_near, j), columns_of(c_near, j)
            row = pl.multiple_of((base + j) * states, states)
            fold = pl.multiple_of((base + j) * SUB, SUB)
            to_entry, to_read = [None] * len(halves), [None] * len(halves)
            for l, lanes in enumerate(slices):
                dt = row_of(dt_rows, base + j, l)
                u = row_of(u_rows, base + j, l)
                grad = row_of(grad_rows, base + j, l)
                inward, recall = None, None
                for h in range(len(halves)):
                    adjoint = read[h] * grad + near[l][h]
                    passed = factors[pl.ds(row + h * SUB, SUB), lanes] * adjoint
                    before = levels[pl.ds(row + h * SUB, SUB), lanes]
                    kept = passed * before
                    rate_sum[l][h] = rate_sum[l][h] + kept * dt
                    one, two = adjoint * entry[h], kept * rates[l][h]
                    inward = one if inward is None else inward + one
                    recall = two if recall is None else recall + two
                    one, two = adjoint * u, level[l][h] * grad
                    to_entry[h] = one if to_entry[h] is None else to_entry[h] + one
                    to_read[h] = two if to_read[h] is None else to_read[h] + two
                    near[l][h] = passed
                    level[l][h] = before
                weighted[l, pl.ds(fold, SUB), :] = inward
                memory[l, pl.ds(fold, SUB), :] = recall
            for h in range(len(halves)):
                entry_part[pl.ds(row + h * SUB, SUB), :] = to_entry[h]
                read_part[pl.ds(row + h * SUB, SUB), :] = to_read[h]
        return tuple(tuple(tuple(one) for one in part) for part in (near, level, rate_sum))

    ahead_now = tuple(tuple(ahead[h, l] for h in halves) for l in slices)
    sums_now = tuple(tuple(rate_grad_ref[h, l] for h in halves) for l in slices)
    near, _, rate_sum = lax.fori_loop(0, steps // SUB, fall, (ahead_now, top, sums_now))
    for l, lanes in enumerate(slices):
        for h, rows in enumerate(halves):
            ahead[rows, lanes] = near[l][h]
            rate_grad_ref[rows, lanes] = rate_sum[l][h]
        inward = fold_rows(weighted, steps, l)
        conv_ref[:, lanes] = inward * dt_ref[:, lanes]
        step_ref[:, lanes] = inward * x_ref[:, lanes].astype(F32) + LN2 * fold_rows(
            memory, steps, l
        )
    ones = jnp.ones((SUB, LANES), F32)
    entry_ref[0] = against(ones, entry_part[...])
    read_ref[0] = against(ones, read_part[...])


def scanned_back(dt, x, grad, entry_t, read_t, rate, starts):
    length, width = dt.shape
    states = rate.shape[0]
    block = TIME_BLOCK
    count = length // block
    last = count - 1
    groups = width // LANES
    by_time = pl.BlockSpec((block, width), lambda i: (last - i, 0))
    across = pl.BlockSpec((states, block), lambda i: (0, last - i))
    fixed = pl.BlockSpec((states, width), lambda i: (0, 0))
    flat = pl.BlockSpec((1, SUB, block * states), lambda i: (last - i, 0, 0))
    conv, step, entry, read, rate_grad = pl.pallas_call(
        back_kernel,
        grid=(count,),
        in_specs=[
            by_time,
            by_time,
            by_time,
            across,
            across,
            fixed,
            pl.BlockSpec((1, states, width), lambda i: (last - i, 0, 0)),
        ],
        out_specs=[by_time, by_time, flat, flat, fixed],
        out_shape=[
            jax.ShapeDtypeStruct((length, width), F32),
            jax.ShapeDtypeStruct((length, width), F32),
            jax.ShapeDtypeStruct((count, SUB, block * states), F32),
            jax.ShapeDtypeStruct((count, SUB, block * states), F32),
            jax.ShapeDtypeStruct((states, width), F32),
        ],
        scratch_shapes=[
            pltpu.VMEM((states, width), F32),
            pltpu.VMEM((groups, block, LANES), F32),
            pltpu.VMEM((groups, block, LANES), F32),
            pltpu.VMEM((groups, block, LANES), F32),
            pltpu.VMEM((block * states, width), F32),
            pltpu.VMEM(((block + 1) * states, width), F32),
            pltpu.VMEM((groups, block * SUB, LANES), F32),
            pltpu.VMEM((groups, block * SUB, LANES), F32),
            pltpu.VMEM((block * states, LANES), F32),
            pltpu.VMEM((block * states, LANES), F32),
        ],
        name="scan_backward",
    )(dt, x, grad, entry_t, read_t, rate, starts)
    entry = entry[:, 0, :].reshape(length, states)
    read = read[:, 0, :].reshape(length, states)
    return conv, step, entry, read, rate_grad


def shards(
    tokens,
    norm_gain,
    inner_weight,
    gate_weight,
    conv_weight,
    conv_bias,
    select_weight,
    step_weight,
    step_bias,
    log_decay,
    skip_gain,
    out_weight,
    cotangent,
):
    local_len, part_width = tokens.shape[1:]
    core = lax.axis_index("ctx")
    seat = lax.axis_index("dp")
    place = lax.axis_index("tensor")
    peers = lax.axis_size("tensor")
    seats = lax.axis_size("dp")
    kernel = conv_weight.shape[0]
    states = log_decay.shape[0]
    half = conv_weight.shape[1] // 2
    order = place ^ jnp.arange(peers, dtype=jnp.int32)

    own_tokens = tokens[0]
    own_cot = cotangent[0]

    def core_rows(weight):
        other = swap(half_of(weight, 1 - core, 1), "ctx", 1)
        return in_order(half_of(weight, core, 1), other, core, 0)

    inner_rows, gate_rows, out_rows, select_rows, step_rows = (
        core_rows(weight)
        for weight in (inner_weight, gate_weight, out_weight.T, select_weight, step_weight)
    )

    def whole(rows):
        full = stacked(gather_pieces(rows, "dp"), "dp")
        return full.reshape((-1,) + rows.shape[1:])

    w_inner = whole(inner_rows)
    w_select = whole(select_rows)
    w_step = whole(step_rows)
    w_gate = whole(gate_rows)
    w_out = whole(out_rows)
    rank_width = w_step.shape[0]
    model_width = w_inner.shape[0]

    token_pieces = gather_pieces(own_tokens, "tensor")
    gain_pieces = gather_pieces(norm_gain[None], "tensor")
    normed_half, inverse_rms = normalized(token_pieces, gain_pieces, order)
    normed = in_order(normed_half, swap(normed_half, "ctx", 1), core, 0)
    cot_half = assembled(gather_pieces(own_cot, "tensor"), order)
    cot = in_order(cot_half, swap(cot_half, "ctx", 1), core, 0)
    length = normed.shape[0]

    own_conv_weight = half_of(conv_weight, core, 1)
    own_conv_bias = half_of(conv_bias, core, 0)
    own_step_bias = half_of(step_bias, core, 0)
    own_skip = half_of(skip_gain, core, 0)
    decay_rate = -jnp.exp(half_of(log_decay, core, 1))

    inner_act = matmul(normed, w_inner).astype(BF16)
    gate_act = matmul(normed, w_gate)
    extended = jnp.pad(inner_act, ((kernel - 1, 0), (0, 0))).astype(F32)
    conv_pre = own_conv_bias + own_conv_weight[0] * extended[0:length]
    for offset in range(1, kernel):
        conv_pre = conv_pre + own_conv_weight[offset] * extended[offset : offset + length]
    conv_low = jax.nn.silu(conv_pre).astype(BF16)

    def summed(terms):
        mine = half_of(terms, core, 0) + swap(half_of(terms, 1 - core, 0), "ctx", 1)
        total = everyone_sum(mine.astype(BF16), "tensor")
        return in_order(total, swap(total, "ctx", 1), core, 0)

    projected = summed(against(conv_low, w_select))
    step_in = projected[:, :rank_width].astype(BF16)
    maps_t = projected[:, rank_width:].T
    entry_t, read_t = maps_t[:states], maps_t[states:]
    step_arg = matmul(step_in, w_step) + own_step_bias
    step_size = jax.nn.softplus(step_arg)
    conv_wide = conv_low.astype(F32)
    rate2 = decay_rate * LOG2E

    local_out, starts = scanned(step_size, conv_low, entry_t, read_t, rate2)
    scan_out = local_out + own_skip * conv_wide
    gate_silu = jax.nn.silu(gate_act)
    gated = (scan_out * gate_silu).astype(BF16)

    def weight_sum(terms):
        rows = terms.shape[0] // seats
        terms = terms.astype(BF16)
        total = exchange_sum(
            lambda j: lax.dynamic_slice_in_dim(terms, j * rows, rows, 0), "dp"
        )
        other = swap(half_of(total, 1 - core, 0), "ctx", 1)
        return in_order(half_of(total, core, 0), other, core, 1)

    def feature_sum(terms):
        terms = terms.astype(BF16)
        mine = half_of(terms, core, 0).astype(F32) + swap(
            half_of(terms, 1 - core, 0), "ctx", 1
        ).astype(F32)
        mine = mine.astype(BF16)
        return exchange_sum(
            lambda j: lax.dynamic_slice_in_dim(mine, j * part_width, part_width, 1), "tensor"
        )

    out_weight_grad = weight_sum(contract(cot, gated)).T
    layer_out = own_tokens.astype(F32) + feature_sum(against(gated, w_out))

    gated_grad = matmul(cot, w_out)
    y_grad = gated_grad * gate_silu
    gate_low = (gated_grad * scan_out * silu_slope(gate_act)).astype(BF16)
    skip_local = jnp.sum(y_grad * conv_wide, axis=0)
    gate_weight_grad = weight_sum(contract(normed, gate_low))

    scan_conv_grad, step_grad, entry_grad, read_grad, rate_grad = scanned_back(
        step_size, conv_low, y_grad, entry_t, read_t, rate2, starts
    )
    step_arg_grad = step_grad * jax.nn.sigmoid(step_arg)
    step_bias_local = jnp.sum(step_arg_grad, axis=0)
    step_low = step_arg_grad.astype(BF16)
    step_weight_local = contract(step_in, step_low)
    proj_terms = jnp.concatenate([against(step_low, w_step), entry_grad, read_grad], axis=1)
    proj_grad = summed(proj_terms).astype(BF16)
    select_local = contract(proj_grad, conv_low)
    conv_out_grad = scan_conv_grad + y_grad * own_skip + matmul(proj_grad, w_select)
    conv_pre_grad = conv_out_grad * silu_slope(conv_pre)
    conv_bias_local = jnp.sum(conv_pre_grad, axis=0)
    conv_weight_local = [
        jnp.sum(conv_pre_grad * extended[offset : offset + length], axis=0)
        for offset in range(kernel)
    ]
    padded = jnp.pad(conv_pre_grad, ((0, kernel - 1), (0, 0)))
    inner_grad = own_conv_weight[0] * padded[kernel - 1 : kernel - 1 + length]
    for offset in range(1, kernel):
        begin = kernel - 1 - offset
        inner_grad = inner_grad + own_conv_weight[offset] * padded[begin : begin + length]
    inner_low = inner_grad.astype(BF16)
    inner_weight_grad = weight_sum(contract(normed, inner_low))
    select_weight_grad = weight_sum(select_local)
    step_weight_grad = weight_sum(step_weight_local)

    normed_terms = against(inner_low, w_inner) + against(gate_low, w_gate)
    normed_grad = feature_sum(normed_terms)
    own_x = own_tokens.astype(F32)
    own_gain = norm_gain.astype(F32)
    token_dots = everyone_sum(
        jnp.sum(normed_grad * own_gain * own_x, axis=-1)[None], "tensor"
    ).reshape(local_len, 1)
    cubed = inverse_rms * inverse_rms * inverse_rms
    tokens_grad = (
        own_cot.astype(F32)
        + inverse_rms * own_gain * normed_grad
        - own_x * cubed * token_dots / model_width
    )
    gain_local = jnp.sum(normed_grad * own_x * inverse_rms, axis=0)[None]
    gain_local = everyone_sum(gain_local, "dp")
    gain_grad = (gain_local + swap(gain_local, "ctx", 1))[0]

    rows = jnp.concatenate(
        [
            jnp.stack(conv_weight_local + [conv_bias_local, step_bias_local, skip_local]),
            rate_grad * decay_rate,
        ],
        axis=0,
    )
    rows = everyone_sum(rows, "dp")
    rows = in_order(rows, swap(rows, "ctx", 1), core, 1)
    return (
        layer_out[None],
        tokens_grad[None],
        gain_grad,
        inner_weight_grad,
        gate_weight_grad,
        rows[:kernel],
        rows[kernel],
        select_weight_grad,
        step_weight_grad,
        rows[kernel + 1],
        rows[kernel + 3 :],
        rows[kernel + 2],
        out_weight_grad,
    )


def solution(mesh):
    return jax.shard_map(
        shards,
        mesh=mesh,
        in_specs=(
            P("dp", "ctx", "tensor"),
            P("tensor"),
            P(("dp", "ctx"), "tensor"),
            P(("dp", "ctx"), "tensor"),
            P(None, "tensor"),
            P("tensor"),
            P(("dp", "ctx"), "tensor"),
            P(("dp", "ctx"), "tensor"),
            P("tensor"),
            P(None, "tensor"),
            P("tensor"),
            P("tensor", ("dp", "ctx")),
            P("dp", "ctx", "tensor"),
        ),
        out_specs=(
            P("dp", "ctx", "tensor"),
            P("dp", "ctx", "tensor"),
            P("tensor"),
            P(("dp", "ctx"), "tensor"),
            P(("dp", "ctx"), "tensor"),
            P(None, "tensor"),
            P("tensor"),
            P(("dp", "ctx"), "tensor"),
            P(("dp", "ctx"), "tensor"),
            P("tensor"),
            P(None, "tensor"),
            P("tensor"),
            P("tensor", ("dp", "ctx")),
        ),
        check_vma=False,
    )
```

time: 1740 us -> 585 us (0.34)
  other arithmetic: 493 us -> 34.7 us
  waiting for transfers between devices: 626 us -> 229 us
  local copies, waits for them, and re-layouts: 391 us -> 39.8 us
  starting transfers between devices: 7.19 us -> 131 us
  blocking collectives: 118 us -> 0 us
  Pallas kernels: 0 us -> 105 us
  matrix products: 75.4 us -> 37.8 us
    reduce_scatter x5 -> x0, waiting for transfers between devices: 358 us -> none  [the longest x1 91 us: shards(): lax.psum_scatter(inner_full, ('dp', 'ctx'), scatter_dimension=0, tiled=True)]
    ppermute x2 -> x80, waiting for transfers between devices: 0.01 us -> 229 us  [swap(): return lax.ppermute(value, axis, [(i, i ^ offset) for i in range(peers)])]
    all_gather x5 -> x0, waiting for transfers between devices: 177 us -> none  [the longest x1 49.3 us: shards(): lax.all_gather(out_weight, ('dp', 'ctx'), axis=1, tiled=True)]
    reduce_sum x6 -> x2, other arithmetic: 142 us -> 3.53 us  [the longest x1 2 us: shards(): jnp.sum(conv_pre_grad * extended[offset:offset + length], axis=0)]
    unnamed x35 -> x0, other arithmetic: 135 us -> none
    add x14 -> x11, other arithmetic: 136 us -> 5.31 us  [the longest x5 4.51 us: exchange_sum(): total = total + swap(blocks_of(me ^ k), axis, k).astype(F32)]
    ppermute x2 -> x80, starting transfers between devices: 3.87 us -> 131 us  [swap(): return lax.ppermute(value, axis, [(i, i ^ offset) for i in range(peers)])]
    slice x23 -> x6, local copies, waits for them, and re-layouts: 132 us -> 4.8 us  [the longest x1 2.14 us: scanned_back(): read = read[:, 0, :].reshape(length, states)]
  transfers between devices with their start and end apart: 17 -> 80, of which waited for: 14 -> 35; matrix products, arithmetic and copies ran while one was open for 5% -> 15% of each run, Pallas kernels for 0% -> 2%
where the time goes in v1:
time: 585 us; the launch traced here: 580 us
  waiting for transfers between devices  229 us (39%)
  starting transfers between devices  131 us (22%)
  Pallas kernels  105 us (18%)
  local copies, waits for them, and re-layouts  39.8 us (7%)
  matrix products  37.8 us (6%)
  other arithmetic  34.7 us (6%)
    ppermute x80, waiting for transfers between devices, swap(): return lax.ppermute(value, axis, [(i, i ^ offset) for i in range(peers)])  229 us
    ppermute x80, starting transfers between devices, swap(): return lax.ppermute(value, axis, [(i, i ^ offset) for i in range(peers)])  131 us
    pallas_call x1, Pallas kernels, scanned_back(): pl.pallas_call(back_kernel, grid=(count,), in_specs=[by_time, by_time, by...  65.7 us
    pallas_call x1, Pallas kernels, scanned(): pl.pallas_call(scan_kernel, grid=(count,), in_specs=[by_time, by_time, ac...  29.5 us
    dot_general x5, matrix products, matmul(): return jnp.dot(operand, partner, preferred_element_type=F32)  17.8 us
  transfers between devices with their start and end apart: 80, of which 35 were waited for; matrix products, arithmetic and copies ran while one was open for 15% of the time, Pallas kernels for 2%

profile of v1, /device:TPU:0, one launch (start us, length us, event | category | flops | bytes accessed | tf_op | source)
XLA Modules:
  0.0 579.9 jit_solution(10416813749815554869)
XLA Ops:
  1.4 3.9 collective-permute-start.5
  19.1 2.8 collective-permute-start.13
  25.0 3.2 collective-permute-start.14
  28.1 2.8 collective-permute-done.14
  39.3 9.8 %collective-permute-done.37.refs_2_ = bf16[512,512]{1,0:T(8,128)(2,1)S(1)} collective-permute-done((bf16[512,512]{1,0:T(8,128)(2,1)S(1)}, bf16[512,512]{1,0:T(8,128)(2,1)S(1)}, u32[]{:S(2)}, u32[]{:S(2)}) %collective-permute-start.37) | collective-permute-done | bytes 524320 | tf_op jit(solution)/shard_map/ppermute | solution.py:43
  54.3 6.0 %collective-permute-done.2.refs_3_ = bf16[512,512]{1,0:T(8,128)(2,1)S(1)} collective-permute-done((bf16[512,512]{1,0:T(8,128)(2,1)S(1)}, bf16[512,512]{1,0:T(8,128)(2,1)S(1)}, u32[]{:S(2)}, u32[]{:S(2)}) %collective-permute-start.2) | collective-permute-done | bytes 524320 | tf_op jit(solution)/shard_map/ppermute | solution.py:43
  61.9 5.0 assemble.1
  66.9 2.7 collective-permute-done.1.refs_2_
  71.3 5.2 normalize.1
  77.8 13.1 %collective-permute-done.9 = bf16[512,512]{1,0:T(8,128)(2,1)} collective-permute-done((bf16[512,512]{1,0:T(8,128)(2,1)}, bf16[512,512]{1,0:T(8,128)(2,1)}, u32[]{:S(2)}, u32[]{:S(2)}) %collective-permute-start.9) | collective-permute-done | bytes 524320 | tf_op jit(solution)/shard_map/ppermute | solution.py:43
  93.3 6.4 %collective-permute-done.25 = bf16[512,512]{1,0:T(8,128)(2,1)S(1)} collective-permute-done((bf16[512,512]{1,0:T(8,128)(2,1)}, bf16[512,512]{1,0:T(8,128)(2,1)S(1)}, u32[]{:S(2)}, u32[]{:S(2)}) %collective-permute-start.25) | collective-permute-done | bytes 524320 | tf_op jit(solution)/shard_map/ppermute | solution.py:43
  99.7 26.6 %collective-permute-start.29 = (bf16[512,512]{1,0:T(8,128)(2,1)S(1)}, bf16[512,512]{1,0:T(8,128)(2,1)S(1)}, u32[]{:S(2)}, u32[]{:S(2)}) collective-permute-start(bf16[512,512]{1,0:T(8,128)(2,1)S(1)} %maximum_select_fusion.14), channel_id=1, source_target_pairs={{0,8},{8,0},{16,24},{24,16},{1,9},{9,1},{17,25},{25,17},{2,10},{10... | collective-permute-start | bytes 1572872 | tf_op jit(solution)/shard_map/ppermute | solution.py:43
  126.4 11.6 %collective-permute-done.26 = bf16[512,512]{1,0:T(8,128)(2,1)S(1)} collective-permute-done((bf16[512,512]{1,0:T(8,128)(2,1)}, bf16[512,512]{1,0:T(8,128)(2,1)S(1)}, u32[]{:S(2)}, u32[]{:S(2)}) %collective-permute-start.26) | collective-permute-done | bytes 524320 | tf_op jit(solution)/shard_map/ppermute | solution.py:43
  138.2 7.6 %collective-permute-done.29 = bf16[512,512]{1,0:T(8,128)(2,1)S(1)} collective-permute-done((bf16[512,512]{1,0:T(8,128)(2,1)S(1)}, bf16[512,512]{1,0:T(8,128)(2,1)S(1)}, u32[]{:S(2)}, u32[]{:S(2)}) %collective-permute-start.29) | collective-permute-done | bytes 524320 | tf_op jit(solution)/shard_map/ppermute | solution.py:43
  145.7 26.6 %collective-permute-start.22 = (bf16[32,512]{1,0:T(8,128)(2,1)S(1)}, bf16[32,512]{1,0:T(8,128)(2,1)S(1)}, u32[]{:S(2)}, u32[]{:S(2)}) collective-permute-start(bf16[32,512]{1,0:T(8,128)(2,1)S(1)} %maximum_select_fusion.21), channel_id=1, source_target_pairs={{0,16},{8,24},{16,0},{24,8},{1,17},{9,25},{17,1},{25,9},{2,18},{10... | collective-permute-start | bytes 98312 | tf_op jit(solution)/shard_map/ppermute | solution.py:43
  172.4 9.7 %collective-permute-done.30 = bf16[512,512]{1,0:T(8,128)(2,1)S(1)} collective-permute-done((bf16[512,512]{1,0:T(8,128)(2,1)S(1)}, bf16[512,512]{1,0:T(8,128)(2,1)S(1)}, u32[]{:S(2)}, u32[]{:S(2)}) %collective-permute-start.30) | collective-permute-done | bytes 524320 | tf_op jit(solution)/shard_map/ppermute | solution.py:43
  187.5 8.8 %fusion.1 = (f32[512]{0:T(512)}, f32[1024,512]{1,0:T(8,128)}, bf16[1024,512]{1,0:T(8,128)(2,1)S(1)}, f32[1024,512]{1,0:T(8,128)}, f32[1024,512]{1,0:T(8,128)}) fusion(f32[1024,512]{1,0:T(8,128)S(1)} %fusion.32, f32[1027,512]{1,0:T(8,128)S(1)} %pad_convert_fusion, f32[512]{0:T(512)S(1)} %bitcast.138, f32[512]{0:T(512)S(1)} %bitcast.134, ...), kind=kOutput, calls=%fused_computation.13 | convolution fusion | flops 2177367552 | bytes 24129536 | tf_op jit(solution)/shard_map/dot_general | solution.py:38
  198.6 3.5 collective-permute-start.18
  202.8 4.4 collective-permute-done.18
  207.2 3.2 collective-permute-done.17
  213.0 3.3 compare_select_fusion
  216.3 29.5 %scan_forward.1 = (f32[1024,512]{1,0:T(8,128)}, f32[8,16,512]{2,1,0:T(8,128)}) custom-call(f32[1024,512]{1,0:T(8,128)} %get-tuple-element.129.dt_ref, bf16[1024,512]{1,0:T(8,128)(2,1)} %copy-done, f32[16,1024]{1,0:T(8,128)} %get-tuple-element.112.bt_ref, f32[16,1024]{1,0:T(8,128)} %get-tuple-element.111.ct_ref, f32[16,512]{1,0:T(8,128)} %fusion.27.rate_ref), custom_call_target="tpu_custom_call" | custom-call | tf_op jit(solution)/shard_map/scan_forward/pallas_call | solution.py:236
  245.8 65.7 %scan_backward.1 = (f32[1024,512]{1,0:T(8,128)}, f32[1024,512]{1,0:T(8,128)}, f32[8,8,2048]{2,1,0:T(8,128)}, f32[8,8,2048]{2,1,0:T(8,128)}, f32[16,512]{1,0:T(8,128)}) custom-call(f32[1024,512]{1,0:T(8,128)} %get-tuple-element.129.dt_ref, bf16[1024,512]{1,0:T(8,128)(2,1)} %copy-done, f32[1024,512]{1,0:T(8,128)} %get-tuple-element.67.grad_ref, ...), custom_call_target="tpu_custom_call" | custom-call | tf_op jit(solution)/shard_map/scan_backward/pallas_call | solution.py:387
  311.5 3.6 fusion.35
  321.8 2.8 convolution_convert_fusion.1
  325.9 9.8 %collective-permute-start.76 = (bf16[512,512]{0,1:T(8,128)(2,1)}, bf16[512,512]{0,1:T(8,128)(2,1)}, u32[]{:S(2)}, u32[]{:S(2)}) collective-permute-start(bf16[512,512]{0,1:T(8,128)(2,1)} %get-tuple-element.75), channel_id=1, source_target_pairs={{0,8},{8,0},{16,24},{24,16},{1,9},{9,1},{17,25},{25,17},{2,10},{10... | collective-permute-start | bytes 1572872 | tf_op jit(solution)/shard_map/ppermute | solution.py:43
  338.4 3.4 collective-permute-start.74
  350.4 4.4 fusion.39
  354.9 3.0 convolution_convert_fusion.2
  357.9 2.6 collective-permute-done.72
  361.7 2.6 collective-permute-done.73
  368.3 4.6 collective-permute-done.43
  380.1 6.7 %collective-permute-done.77 = bf16[512,512]{0,1:T(8,128)(2,1)S(1)} collective-permute-done((bf16[512,512]{0,1:T(8,128)(2,1)S(1)}, bf16[512,512]{0,1:T(8,128)(2,1)S(1)}, u32[]{:S(2)}, u32[]{:S(2)}) %collective-permute-start.77) | collective-permute-done | bytes 524320 | tf_op jit(solution)/shard_map/ppermute | solution.py:43
  389.6 18.7 %collective-permute-done.60 = bf16[512,512]{0,1:T(8,128)(2,1)S(1)} collective-permute-done((bf16[512,512]{0,1:T(8,128)(2,1)S(1)}, bf16[512,512]{0,1:T(8,128)(2,1)S(1)}, u32[]{:S(2)}, u32[]{:S(2)}) %collective-permute-start.60) | collective-permute-done | bytes 524320 | tf_op jit(solution)/shard_map/ppermute | solution.py:43
  408.3 22.5 %collective-permute-done.61 = bf16[512,512]{0,1:T(8,128)(2,1)S(1)} collective-permute-done((bf16[512,512]{0,1:T(8,128)(2,1)S(1)}, bf16[512,512]{0,1:T(8,128)(2,1)S(1)}, u32[]{:S(2)}, u32[]{:S(2)}) %collective-permute-start.61) | collective-permute-done | bytes 524320 | tf_op jit(solution)/shard_map/ppermute | solution.py:43
  444.5 2.6 convolution_convert_fusion.3
  453.1 3.7 collective-permute-done.66
  458.3 2.6 collective-permute-done.64
  471.8 2.7 fusion.12
  474.5 4.1 collective-permute-done.56
  478.6 11.9 %collective-permute-done.58 = bf16[512,512]{0,1:T(8,128)(2,1)} collective-permute-done((bf16[512,512]{0,1:T(8,128)(2,1)}, bf16[512,512]{0,1:T(8,128)(2,1)}, u32[]{:S(2)}, u32[]{:S(2)}) %collective-permute-start.58) | collective-permute-done | bytes 524320 | tf_op jit(solution)/shard_map/ppermute | solution.py:43
  490.5 22.5 %collective-permute-done.57 = bf16[512,512]{0,1:T(8,128)(2,1)} collective-permute-done((bf16[512,512]{0,1:T(8,128)(2,1)}, bf16[512,512]{0,1:T(8,128)(2,1)}, u32[]{:S(2)}, u32[]{:S(2)}) %collective-permute-start.57) | collective-permute-done | bytes 524320 | tf_op jit(solution)/shard_map/ppermute | solution.py:43
  522.1 8.8 %collective-permute-done.46 = bf16[512,512]{1,0:T(8,128)(2,1)S(1)} collective-permute-done((bf16[512,512]{1,0:T(8,128)(2,1)S(1)}, bf16[512,512]{1,0:T(8,128)(2,1)S(1)}, u32[]{:S(2)}, u32[]{:S(2)}) %collective-permute-start.46) | collective-permute-done | bytes 524320 | tf_op jit(solution)/shard_map/ppermute | solution.py:43
  530.9 11.8 %collective-permute-done.48 = bf16[512,512]{1,0:T(8,128)(2,1)S(1)} collective-permute-done((bf16[512,512]{1,0:T(8,128)(2,1)S(1)}, bf16[512,512]{1,0:T(8,128)(2,1)S(1)}, u32[]{:S(2)}, u32[]{:S(2)}) %collective-permute-start.48) | collective-permute-done | bytes 524320 | tf_op jit(solution)/shard_map/ppermute | solution.py:43
  553.5 2.7 collective-permute-start.52
  557.2 2.5 copy.36
  561.8 13.6 %collective-permute-done.50 = f32[1,512]{1,0:T(1,128)S(1)} collective-permute-done((f32[1,512]{1,0:T(1,128)S(1)}, f32[1,512]{1,0:T(1,128)S(1)}, u32[]{:S(2)}, u32[]{:S(2)}) %collective-permute-start.50) | collective-permute-done | bytes 2080 | tf_op jit(solution)/shard_map/ppermute | solution.py:43
  575.4 3.6 fusion.8
  (394 shorter events, 138.5 us)
Async XLA Ops:
  1.4 20.5 %collective-permute-start.5 = (bf16[1,512]{1,0:T(2,128)(2,1)S(1)}, bf16[1,512]{1,0:T(2,128)(2,1)S(1)}, u32[]{:S(2)}, u32[]{:S(2)}) collective-permute-start(bf16[1,512]{1,0:T(2,128)(2,1)S(1)} %broadcast_in_dim.77.refs_4_), channel_id=1, source_target_pairs={{0,3},{1,2},{2,1},{3,0},{4,7},{5,6},{6,5},{7,4},{8,11},{9,10},{10,... | collective-permute-start | bytes 3080 | tf_op jit(solution)/shard_map/ppermute | solution.py:43
  5.3 19.1 %collective-permute-start.4 = (bf16[1,512]{1,0:T(2,128)(2,1)S(1)}, bf16[1,512]{1,0:T(2,128)(2,1)S(1)}, u32[]{:S(2)}, u32[]{:S(2)}) collective-permute-start(bf16[1,512]{1,0:T(2,128)(2,1)S(1)} %broadcast_in_dim.77.refs_4_), channel_id=1, source_target_pairs={{0,2},{1,3},{2,0},{3,1},{4,6},{5,7},{6,4},{7,5},{8,10},{9,11},{10,... | collective-permute-start | bytes 3080 | tf_op jit(solution)/shard_map/ppermute | solution.py:43
  5.8 19.1 %collective-permute-start.3 = (bf16[1,512]{1,0:T(2,128)(2,1)S(1)}, bf16[1,512]{1,0:T(2,128)(2,1)S(1)}, u32[]{:S(2)}, u32[]{:S(2)}) collective-permute-start(bf16[1,512]{1,0:T(2,128)(2,1)S(1)} %broadcast_in_dim.77.refs_4_), channel_id=1, source_target_pairs={{0,1},{1,0},{2,3},{3,2},{4,5},{5,4},{6,7},{7,6},{8,9},{9,8},{10,11... | collective-permute-start | bytes 3080 | tf_op jit(solution)/shard_map/ppermute | solution.py:43
  14.8 16.8 %collective-permute-start.7 = (bf16[256,512]{1,0:T(8,128)(2,1)}, bf16[256,512]{1,0:T(8,128)(2,1)S(1)}, u32[]{:S(2)}, u32[]{:S(2)}) collective-permute-start(bf16[256,512]{1,0:T(8,128)(2,1)} %get-tuple-element.100), channel_id=1, source_target_pairs={{0,4},{4,0},{1,5},{5,1},{2,6},{6,2},{3,7},{7,3},{8,12},{12,8},{9,1... | collective-permute-start | bytes 786440 | tf_op jit(solution)/shard_map/ppermute | solution.py:43
  21.9 15.9 %collective-permute-start.38 = (bf16[512,512]{1,0:T(8,128)(2,1)S(1)}, bf16[512,512]{1,0:T(8,128)(2,1)S(1)}, u32[]{:S(2)}, u32[]{:S(2)}) collective-permute-start(bf16[512,512]{1,0:T(8,128)(2,1)S(1)} %bitcast.110), channel_id=1, source_target_pairs={{0,3},{1,2},{2,1},{3,0},{4,7},{5,6},{6,5},{7,4},{8,11},{9,10},{10,... | collective-permute-start | bytes 1572872 | tf_op jit(solution)/shard_map/ppermute | solution.py:43
  24.4 24.6 %collective-permute-start.37 = (bf16[512,512]{1,0:T(8,128)(2,1)S(1)}, bf16[512,512]{1,0:T(8,128)(2,1)S(1)}, u32[]{:S(2)}, u32[]{:S(2)}) collective-permute-start(bf16[512,512]{1,0:T(8,128)(2,1)S(1)} %bitcast.111), channel_id=1, source_target_pairs={{0,2},{1,3},{2,0},{3,1},{4,6},{5,7},{6,4},{7,5},{8,10},{9,11},{10,... | collective-permute-start | bytes 1572872 | tf_op jit(solution)/shard_map/ppermute | solution.py:43
  30.9 20.6 %collective-permute-start.36 = (bf16[512,512]{1,0:T(8,128)(2,1)S(1)}, bf16[512,512]{1,0:T(8,128)(2,1)S(1)}, u32[]{:S(2)}, u32[]{:S(2)}) collective-permute-start(bf16[512,512]{1,0:T(8,128)(2,1)S(1)} %bitcast.112), channel_id=1, source_target_pairs={{0,1},{1,0},{2,3},{3,2},{4,5},{5,4},{6,7},{7,6},{8,9},{9,8},{10,11... | collective-permute-start | bytes 1572872 | tf_op jit(solution)/shard_map/ppermute | solution.py:43
  31.6 28.7 %collective-permute-start.2 = (bf16[512,512]{1,0:T(8,128)(2,1)S(1)}, bf16[512,512]{1,0:T(8,128)(2,1)S(1)}, u32[]{:S(2)}, u32[]{:S(2)}) collective-permute-start(bf16[512,512]{1,0:T(8,128)(2,1)S(1)} %bitcast.102), channel_id=1, source_target_pairs={{0,3},{1,2},{2,1},{3,0},{4,7},{5,6},{6,5},{7,4},{8,11},{9,10},{10,... | collective-permute-start | bytes 1572872 | tf_op jit(solution)/shard_map/ppermute | solution.py:43
  35.0 34.6 %collective-permute-start.1 = (bf16[512,512]{1,0:T(8,128)(2,1)S(1)}, bf16[512,512]{1,0:T(8,128)(2,1)}, u32[]{:S(2)}, u32[]{:S(2)}) collective-permute-start(bf16[512,512]{1,0:T(8,128)(2,1)S(1)} %bitcast.103), channel_id=1, source_target_pairs={{0,2},{1,3},{2,0},{3,1},{4,6},{5,7},{6,4},{7,5},{8,10},{9,11},{10,... | collective-permute-start | bytes 1572872 | tf_op jit(solution)/shard_map/ppermute | solution.py:43
  37.8 33.2 %collective-permute-start = (bf16[512,512]{1,0:T(8,128)(2,1)S(1)}, bf16[512,512]{1,0:T(8,128)(2,1)}, u32[]{:S(2)}, u32[]{:S(2)}) collective-permute-start(bf16[512,512]{1,0:T(8,128)(2,1)S(1)} %bitcast.104), channel_id=1, source_target_pairs={{0,1},{1,0},{2,3},{3,2},{4,5},{5,4},{6,7},{7,6},{8,9},{9,8},{10,11... | collective-permute-start | bytes 1572872 | tf_op jit(solution)/shard_map/ppermute | solution.py:43
  49.1 27.4 %collective-permute-start.8 = (bf16[512,512]{1,0:T(8,128)(2,1)}, bf16[512,512]{1,0:T(8,128)(2,1)}, u32[]{:S(2)}, u32[]{:S(2)}) collective-permute-start(bf16[512,512]{1,0:T(8,128)(2,1)} %maximum_select_fusion.10), channel_id=1, source_target_pairs={{0,8},{8,0},{16,24},{24,16},{1,9},{9,1},{17,25},{25,17},{2,10},{10... | collective-permute-start | bytes 1572872 | tf_op jit(solution)/shard_map/ppermute | solution.py:43
  51.5 39.4 %collective-permute-start.9 = (bf16[512,512]{1,0:T(8,128)(2,1)}, bf16[512,512]{1,0:T(8,128)(2,1)}, u32[]{:S(2)}, u32[]{:S(2)}) collective-permute-start(bf16[512,512]{1,0:T(8,128)(2,1)} %maximum_select_fusion.10), channel_id=1, source_target_pairs={{0,16},{8,24},{16,0},{24,8},{1,17},{9,25},{17,1},{25,9},{2,18},{10... | collective-permute-start | bytes 1572872 | tf_op jit(solution)/shard_map/ppermute | solution.py:43
  60.3 31.7 %collective-permute-start.10 = (bf16[512,512]{1,0:T(8,128)(2,1)}, bf16[512,512]{1,0:T(8,128)(2,1)}, u32[]{:S(2)}, u32[]{:S(2)}) collective-permute-start(bf16[512,512]{1,0:T(8,128)(2,1)} %maximum_select_fusion.10), channel_id=1, source_target_pairs={{0,24},{8,16},{16,8},{24,0},{1,25},{9,17},{17,9},{25,1},{2,26},{10... | collective-permute-start | bytes 1572872 | tf_op jit(solution)/shard_map/ppermute | solution.py:43
  69.6 141.0 %collective-permute-start.23 = (bf16[32,512]{1,0:T(8,128)(2,1)S(1)}, bf16[32,512]{1,0:T(8,128)(2,1)S(1)}, u32[]{:S(2)}, u32[]{:S(2)}) collective-permute-start(bf16[32,512]{1,0:T(8,128)(2,1)S(1)} %maximum_select_fusion.21), channel_id=1, source_target_pairs={{0,24},{8,16},{16,8},{24,0},{1,25},{9,17},{17,9},{25,1},{2,26},{10... | collective-permute-start | bytes 98312 | tf_op jit(solution)/shard_map/ppermute | solution.py:43
  71.0 28.8 %collective-permute-start.25 = (bf16[512,512]{1,0:T(8,128)(2,1)}, bf16[512,512]{1,0:T(8,128)(2,1)S(1)}, u32[]{:S(2)}, u32[]{:S(2)}) collective-permute-start(bf16[512,512]{1,0:T(8,128)(2,1)} %maximum_select_fusion.12), channel_id=1, source_target_pairs={{0,8},{8,0},{16,24},{24,16},{1,9},{9,1},{17,25},{25,17},{2,10},{10... | collective-permute-start | bytes 1572872 | tf_op jit(solution)/shard_map/ppermute | solution.py:43
  76.5 105.8 %collective-permute-start.6 = (bf16[512,2048]{1,0:T(8,128)(2,1)}, bf16[512,2048]{1,0:T(8,128)(2,1)S(1)}, u32[]{:S(2)}, u32[]{:S(2)}) collective-permute-start(bf16[512,2048]{1,0:T(8,128)(2,1)} %get-tuple-element.22), channel_id=1, source_target_pairs={{0,4},{4,0},{1,5},{5,1},{2,6},{6,2},{3,7},{7,3},{8,12},{12,8},{9,1... | collective-permute-start | bytes 6291464 | tf_op jit(solution)/shard_map/ppermute | solution.py:43
  90.9 47.1 %collective-permute-start.26 = (bf16[512,512]{1,0:T(8,128)(2,1)}, bf16[512,512]{1,0:T(8,128)(2,1)S(1)}, u32[]{:S(2)}, u32[]{:S(2)}) collective-permute-start(bf16[512,512]{1,0:T(8,128)(2,1)} %maximum_select_fusion.12), channel_id=1, source_target_pairs={{0,16},{8,24},{16,0},{24,8},{1,17},{9,25},{17,1},{25,9},{2,18},{10... | collective-permute-start | bytes 1572872 | tf_op jit(solution)/shard_map/ppermute | solution.py:43
  92.0 46.0 %collective-permute-start.27 = (bf16[512,512]{1,0:T(8,128)(2,1)}, bf16[512,512]{1,0:T(8,128)(2,1)S(1)}, u32[]{:S(2)}, u32[]{:S(2)}) collective-permute-start(bf16[512,512]{1,0:T(8,128)(2,1)} %maximum_select_fusion.12), channel_id=1, source_target_pairs={{0,24},{8,16},{16,8},{24,0},{1,25},{9,17},{17,9},{25,1},{2,26},{10... | collective-permute-start | bytes 1572872 | tf_op jit(solution)/shard_map/ppermute | solution.py:43
  99.7 46.0 %collective-permute-start.29 = (bf16[512,512]{1,0:T(8,128)(2,1)S(1)}, bf16[512,512]{1,0:T(8,128)(2,1)S(1)}, u32[]{:S(2)}, u32[]{:S(2)}) collective-permute-start(bf16[512,512]{1,0:T(8,128)(2,1)S(1)} %maximum_select_fusion.14), channel_id=1, source_target_pairs={{0,8},{8,0},{16,24},{24,16},{1,9},{9,1},{17,25},{25,17},{2,10},{10... | collective-permute-start | bytes 1572872 | tf_op jit(solution)/shard_map/ppermute | solution.py:43
  138.0 44.2 %collective-permute-start.30 = (bf16[512,512]{1,0:T(8,128)(2,1)S(1)}, bf16[512,512]{1,0:T(8,128)(2,1)S(1)}, u32[]{:S(2)}, u32[]{:S(2)}) collective-permute-start(bf16[512,512]{1,0:T(8,128)(2,1)S(1)} %maximum_select_fusion.14), channel_id=1, source_target_pairs={{0,16},{8,24},{16,0},{24,8},{1,17},{9,25},{17,1},{25,9},{2,18},{10... | collective-permute-start | bytes 1572872 | tf_op jit(solution)/shard_map/ppermute | solution.py:43
  138.0 44.1 %collective-permute-start.31 = (bf16[512,512]{1,0:T(8,128)(2,1)S(1)}, bf16[512,512]{1,0:T(8,128)(2,1)S(1)}, u32[]{:S(2)}, u32[]{:S(2)}) collective-permute-start(bf16[512,512]{1,0:T(8,128)(2,1)S(1)} %maximum_select_fusion.14), channel_id=1, source_target_pairs={{0,24},{8,16},{16,8},{24,0},{1,25},{9,17},{17,9},{25,1},{2,26},{10... | collective-permute-start | bytes 1572872 | tf_op jit(solution)/shard_map/ppermute | solution.py:43
  145.7 57.0 %collective-permute-start.22 = (bf16[32,512]{1,0:T(8,128)(2,1)S(1)}, bf16[32,512]{1,0:T(8,128)(2,1)S(1)}, u32[]{:S(2)}, u32[]{:S(2)}) collective-permute-start(bf16[32,512]{1,0:T(8,128)(2,1)S(1)} %maximum_select_fusion.21), channel_id=1, source_target_pairs={{0,16},{8,24},{16,0},{24,8},{1,17},{9,25},{17,1},{25,9},{2,18},{10... | collective-permute-start | bytes 98312 | tf_op jit(solution)/shard_map/ppermute | solution.py:43
  182.1 15.2 %collective-permute-start.21 = (bf16[32,512]{1,0:T(8,128)(2,1)S(1)}, bf16[32,512]{1,0:T(8,128)(2,1)S(1)}, u32[]{:S(2)}, u32[]{:S(2)}) collective-permute-start(bf16[32,512]{1,0:T(8,128)(2,1)S(1)} %maximum_select_fusion.21), channel_id=1, source_target_pairs={{0,8},{8,0},{16,24},{24,16},{1,9},{9,1},{17,25},{25,17},{2,10},{10... | collective-permute-start | bytes 98312 | tf_op jit(solution)/shard_map/ppermute | solution.py:43
  325.9 53.6 %collective-permute-start.76 = (bf16[512,512]{0,1:T(8,128)(2,1)}, bf16[512,512]{0,1:T(8,128)(2,1)}, u32[]{:S(2)}, u32[]{:S(2)}) collective-permute-start(bf16[512,512]{0,1:T(8,128)(2,1)} %get-tuple-element.75), channel_id=1, source_target_pairs={{0,8},{8,0},{16,24},{24,16},{1,9},{9,1},{17,25},{25,17},{2,10},{10... | collective-permute-start | bytes 1572872 | tf_op jit(solution)/shard_map/ppermute | solution.py:43
  335.7 44.3 %collective-permute-start.78 = (bf16[512,512]{0,1:T(8,128)(2,1)}, bf16[512,512]{0,1:T(8,128)(2,1)}, u32[]{:S(2)}, u32[]{:S(2)}) collective-permute-start(bf16[512,512]{0,1:T(8,128)(2,1)} %get-tuple-element.76), channel_id=1, source_target_pairs={{0,24},{8,16},{16,8},{24,0},{1,25},{9,17},{17,9},{25,1},{2,26},{10... | collective-permute-start | bytes 1572872 | tf_op jit(solution)/shard_map/ppermute | solution.py:43
  338.4 22.1 %collective-permute-start.72 = (bf16[32,512]{1,0:T(8,128)(2,1)}, bf16[32,512]{1,0:T(8,128)(2,1)}, u32[]{:S(2)}, u32[]{:S(2)}) collective-permute-start(bf16[32,512]{1,0:T(8,128)(2,1)} %get-tuple-element.108), channel_id=1, source_target_pairs={{0,8},{8,0},{16,24},{24,16},{1,9},{9,1},{17,25},{25,17},{2,10},{10... | collective-permute-start | bytes 98312 | tf_op jit(solution)/shard_map/ppermute | solution.py:43
  338.4 23.3 %collective-permute-start.74 = (bf16[32,512]{1,0:T(8,128)(2,1)}, bf16[32,512]{1,0:T(8,128)(2,1)}, u32[]{:S(2)}, u32[]{:S(2)}) collective-permute-start(bf16[32,512]{1,0:T(8,128)(2,1)} %get-tuple-element.109), channel_id=1, source_target_pairs={{0,24},{8,16},{16,8},{24,0},{1,25},{9,17},{17,9},{25,1},{2,26},{10... | collective-permute-start | bytes 98312 | tf_op jit(solution)/shard_map/ppermute | solution.py:43
  341.7 22.5 %collective-permute-start.73 = (bf16[32,512]{1,0:T(8,128)(2,1)S(1)}, bf16[32,512]{1,0:T(8,128)(2,1)}, u32[]{:S(2)}, u32[]{:S(2)}) collective-permute-start(bf16[32,512]{1,0:T(8,128)(2,1)S(1)} %get-tuple-element.110), channel_id=1, source_target_pairs={{0,16},{8,24},{16,0},{24,8},{1,17},{9,25},{17,1},{25,9},{2,18},{10... | collective-permute-start | bytes 98312 | tf_op jit(solution)/shard_map/ppermute | solution.py:43
  360.5 26.4 %collective-permute-start.77 = (bf16[512,512]{0,1:T(8,128)(2,1)S(1)}, bf16[512,512]{0,1:T(8,128)(2,1)S(1)}, u32[]{:S(2)}, u32[]{:S(2)}) collective-permute-start(bf16[512,512]{0,1:T(8,128)(2,1)S(1)} %copy-done.34), channel_id=1, source_target_pairs={{0,16},{8,24},{16,0},{24,8},{1,17},{9,25},{17,1},{25,9},{2,18},{10... | collective-permute-start | bytes 1572872 | tf_op jit(solution)/shard_map/ppermute | solution.py:43
  376.3 32.0 %collective-permute-start.60 = (bf16[512,512]{0,1:T(8,128)(2,1)S(1)}, bf16[512,512]{0,1:T(8,128)(2,1)S(1)}, u32[]{:S(2)}, u32[]{:S(2)}) collective-permute-start(bf16[512,512]{0,1:T(8,128)(2,1)S(1)} %get-tuple-element.79), channel_id=1, source_target_pairs={{0,8},{8,0},{16,24},{24,16},{1,9},{9,1},{17,25},{25,17},{2,10},{10... | collective-permute-start | bytes 1572872 | tf_op jit(solution)/shard_map/ppermute | solution.py:43
  378.7 29.6 %collective-permute-start.62 = (bf16[512,512]{0,1:T(8,128)(2,1)S(1)}, bf16[512,512]{0,1:T(8,128)(2,1)S(1)}, u32[]{:S(2)}, u32[]{:S(2)}) collective-permute-start(bf16[512,512]{0,1:T(8,128)(2,1)S(1)} %get-tuple-element.80), channel_id=1, source_target_pairs={{0,24},{8,16},{16,8},{24,0},{1,25},{9,17},{17,9},{25,1},{2,26},{10... | collective-permute-start | bytes 1572872 | tf_op jit(solution)/shard_map/ppermute | solution.py:43
  379.5 51.4 %collective-permute-start.61 = (bf16[512,512]{0,1:T(8,128)(2,1)S(1)}, bf16[512,512]{0,1:T(8,128)(2,1)S(1)}, u32[]{:S(2)}, u32[]{:S(2)}) collective-permute-start(bf16[512,512]{0,1:T(8,128)(2,1)S(1)} %get-tuple-element.81), channel_id=1, source_target_pairs={{0,16},{8,24},{16,0},{24,8},{1,17},{9,25},{17,1},{25,9},{2,18},{10... | collective-permute-start | bytes 1572872 | tf_op jit(solution)/shard_map/ppermute | solution.py:43
  380.0 52.1 %collective-permute-start.44 = (bf16[512,160]{0,1:T(8,128)(2,1)S(1)}, bf16[512,160]{0,1:T(8,128)(2,1)S(1)}, u32[]{:S(2)}, u32[]{:S(2)}) collective-permute-start(bf16[512,160]{0,1:T(8,128)(2,1)S(1)} %convert_add_fusion.5), channel_id=1, source_target_pairs={{0,4},{4,0},{1,5},{5,1},{2,6},{6,2},{3,7},{7,3},{8,12},{12,8},{9,1... | collective-permute-start | bytes 491528 | tf_op jit(solution)/shard_map/ppermute | solution.py:43
  389.6 74.8 %collective-permute-start.79 = (f32[256,512]{0,1:T(8,128)}, f32[256,512]{0,1:T(8,128)}, u32[]{:S(2)}, u32[]{:S(2)}) collective-permute-start(f32[256,512]{0,1:T(8,128)} %get-tuple-element.92), channel_id=1, source_target_pairs={{0,4},{4,0},{1,5},{5,1},{2,6},{6,2},{3,7},{7,3},{8,12},{12,8},{9,1... | collective-permute-start | bytes 1572872 | tf_op jit(solution)/shard_map/ppermute | solution.py:43
  444.5 70.5 %collective-permute-start.45 = (bf16[512,2048]{1,0:T(8,128)(2,1)}, bf16[512,2048]{1,0:T(8,128)(2,1)S(1)}, u32[]{:S(2)}, u32[]{:S(2)}) collective-permute-start(bf16[512,2048]{1,0:T(8,128)(2,1)} %constant_dynamic-slice_fusion.29), channel_id=1, source_target_pairs={{0,4},{4,0},{1,5},{5,1},{2,6},{6,2},{3,7},{7,3},{8,12},{12,8},{9,1... | collective-permute-start | bytes 6291464 | tf_op jit(solution)/shard_map/ppermute | solution.py:43
  450.1 16.0 %collective-permute-start.63 = (f32[256,512]{0,1:T(8,128)S(1)}, f32[256,512]{0,1:T(8,128)S(1)}, u32[]{:S(2)}, u32[]{:S(2)}) collective-permute-start(f32[256,512]{0,1:T(8,128)S(1)} %copy-done.40), channel_id=1, source_target_pairs={{0,4},{4,0},{1,5},{5,1},{2,6},{6,2},{3,7},{7,3},{8,12},{12,8},{9,1... | collective-permute-start | bytes 1572872 | tf_op jit(solution)/shard_map/ppermute | solution.py:43
  458.3 61.3 %collective-permute-start.32 = (bf16[512,2048]{1,0:T(8,128)(2,1)}, bf16[512,2048]{1,0:T(8,128)(2,1)}, u32[]{:S(2)}, u32[]{:S(2)}) collective-permute-start(bf16[512,2048]{1,0:T(8,128)(2,1)} %constant_dynamic-slice_fusion.34), channel_id=1, source_target_pairs={{0,4},{4,0},{1,5},{5,1},{2,6},{6,2},{3,7},{7,3},{8,12},{12,8},{9,1... | collective-permute-start | bytes 6291464 | tf_op jit(solution)/shard_map/ppermute | solution.py:43
  463.8 14.8 %collective-permute-start.56 = (bf16[512,512]{0,1:T(8,128)(2,1)}, bf16[512,512]{0,1:T(8,128)(2,1)}, u32[]{:S(2)}, u32[]{:S(2)}) collective-permute-start(bf16[512,512]{0,1:T(8,128)(2,1)} %get-tuple-element.82), channel_id=1, source_target_pairs={{0,8},{8,0},{16,24},{24,16},{1,9},{9,1},{17,25},{25,17},{2,10},{10... | collective-permute-start | bytes 1572872 | tf_op jit(solution)/shard_map/ppermute | solution.py:43
  464.4 26.1 %collective-permute-start.58 = (bf16[512,512]{0,1:T(8,128)(2,1)}, bf16[512,512]{0,1:T(8,128)(2,1)}, u32[]{:S(2)}, u32[]{:S(2)}) collective-permute-start(bf16[512,512]{0,1:T(8,128)(2,1)} %get-tuple-element.83), channel_id=1, source_target_pairs={{0,24},{8,16},{16,8},{24,0},{1,25},{9,17},{17,9},{25,1},{2,26},{10... | collective-permute-start | bytes 1572872 | tf_op jit(solution)/shard_map/ppermute | solution.py:43
  466.1 46.9 %collective-permute-start.57 = (bf16[512,512]{0,1:T(8,128)(2,1)}, bf16[512,512]{0,1:T(8,128)(2,1)}, u32[]{:S(2)}, u32[]{:S(2)}) collective-permute-start(bf16[512,512]{0,1:T(8,128)(2,1)} %get-tuple-element.84), channel_id=1, source_target_pairs={{0,16},{8,24},{16,0},{24,8},{1,17},{9,25},{17,1},{25,9},{2,18},{10... | collective-permute-start | bytes 1572872 | tf_op jit(solution)/shard_map/ppermute | solution.py:43
  514.9 37.1 %collective-permute-start.59 = (f32[256,512]{0,1:T(8,128)S(1)}, f32[256,512]{0,1:T(8,128)S(1)}, u32[]{:S(2)}, u32[]{:S(2)}) collective-permute-start(f32[256,512]{0,1:T(8,128)S(1)} %get-tuple-element.96), channel_id=1, source_target_pairs={{0,4},{4,0},{1,5},{5,1},{2,6},{6,2},{3,7},{7,3},{8,12},{12,8},{9,1... | collective-permute-start | bytes 1572872 | tf_op jit(solution)/shard_map/ppermute | solution.py:43
  517.6 25.1 %collective-permute-start.48 = (bf16[512,512]{1,0:T(8,128)(2,1)S(1)}, bf16[512,512]{1,0:T(8,128)(2,1)S(1)}, u32[]{:S(2)}, u32[]{:S(2)}) collective-permute-start(bf16[512,512]{1,0:T(8,128)(2,1)S(1)} %get-tuple-element.86), channel_id=1, source_target_pairs={{0,3},{1,2},{2,1},{3,0},{4,7},{5,6},{6,5},{7,4},{8,11},{9,10},{10,... | collective-permute-start | bytes 1572872 | tf_op jit(solution)/shard_map/ppermute | solution.py:43
  519.1 25.0 %collective-permute-start.47 = (bf16[512,512]{1,0:T(8,128)(2,1)S(1)}, bf16[512,512]{1,0:T(8,128)(2,1)S(1)}, u32[]{:S(2)}, u32[]{:S(2)}) collective-permute-start(bf16[512,512]{1,0:T(8,128)(2,1)S(1)} %get-tuple-element.87), channel_id=1, source_target_pairs={{0,2},{1,3},{2,0},{3,1},{4,6},{5,7},{6,4},{7,5},{8,10},{9,11},{10,... | collective-permute-start | bytes 1572872 | tf_op jit(solution)/shard_map/ppermute | solution.py:43
  550.0 25.4 %collective-permute-start.33 = (bf16[512,512]{1,0:T(8,128)(2,1)}, bf16[512,512]{1,0:T(8,128)(2,1)}, u32[]{:S(2)}, u32[]{:S(2)}) collective-permute-start(bf16[512,512]{1,0:T(8,128)(2,1)} %get-tuple-element.88), channel_id=1, source_target_pairs={{0,1},{1,0},{2,3},{3,2},{4,5},{5,4},{6,7},{7,6},{8,9},{9,8},{10,11... | collective-permute-start | bytes 1572872 | tf_op jit(solution)/shard_map/ppermute | solution.py:43
  550.6 24.8 %collective-permute-start.35 = (bf16[512,512]{1,0:T(8,128)(2,1)}, bf16[512,512]{1,0:T(8,128)(2,1)}, u32[]{:S(2)}, u32[]{:S(2)}) collective-permute-start(bf16[512,512]{1,0:T(8,128)(2,1)} %get-tuple-element.89), channel_id=1, source_target_pairs={{0,3},{1,2},{2,1},{3,0},{4,7},{5,6},{6,5},{7,4},{8,11},{9,10},{10,... | collective-permute-start | bytes 1572872 | tf_op jit(solution)/shard_map/ppermute | solution.py:43
  552.0 23.4 %collective-permute-start.34 = (bf16[512,512]{1,0:T(8,128)(2,1)}, bf16[512,512]{1,0:T(8,128)(2,1)}, u32[]{:S(2)}, u32[]{:S(2)}) collective-permute-start(bf16[512,512]{1,0:T(8,128)(2,1)} %get-tuple-element.90), channel_id=1, source_target_pairs={{0,2},{1,3},{2,0},{3,1},{4,6},{5,7},{6,4},{7,5},{8,10},{9,11},{10,... | collective-permute-start | bytes 1572872 | tf_op jit(solution)/shard_map/ppermute | solution.py:43
  559.8 15.6 %collective-permute-start.50 = (f32[1,512]{1,0:T(1,128)S(1)}, f32[1,512]{1,0:T(1,128)S(1)}, u32[]{:S(2)}, u32[]{:S(2)}) collective-permute-start(f32[1,512]{1,0:T(1,128)S(1)} %bitcast.142), channel_id=1, source_target_pairs={{0,2},{1,3},{2,0},{3,1},{4,6},{5,7},{6,4},{7,5},{8,10},{9,11},{10,... | collective-permute-start | bytes 6152 | tf_op jit(solution)/shard_map/ppermute | solution.py:43
  560.4 15.0 %collective-permute-start.49 = (f32[1,512]{1,0:T(1,128)S(1)}, f32[1,512]{1,0:T(1,128)S(1)}, u32[]{:S(2)}, u32[]{:S(2)}) collective-permute-start(f32[1,512]{1,0:T(1,128)S(1)} %bitcast.143), channel_id=1, source_target_pairs={{0,1},{1,0},{2,3},{3,2},{4,5},{5,4},{6,7},{7,6},{8,9},{9,8},{10,11... | collective-permute-start | bytes 6152 | tf_op jit(solution)/shard_map/ppermute | solution.py:43
  (111 other events, 2340.3 us)
